TPU v7x, 32 devices: a whole 2x2x4 slice. The times are simulated.
32 devices in a mesh: head: 2 (over y), inner: 4 (over x, core), outer: 4 (over z).
Axes of the slice: x: 2, y: 2, z: 4, core: 2. Of those that a mesh axis runs over, the one named last changes fastest.
Arguments:
- queries: bfloat16 [16, 128, 4096], P(('inner', 'outer'), None, 'head'), may hold values from -2.5 to 2.5
- keys: bfloat16 [16, 128, 512], P(('inner', 'outer'), None, 'head'), may hold values from -2.5 to 2.5
- values: bfloat16 [16, 128, 512], P(('inner', 'outer'), None, 'head'), may hold values from -4 to 4
- grad_out: bfloat16 [16, 128, 4096], P(('inner', 'outer'), None, 'head'), may hold values from -4 to 4
- log_denominator: float32 [16, 128, 32], P(('inner', 'outer'), None, 'head'), may hold values from 6 to 9
- output_row_dot: float32 [16, 128, 32], P(('inner', 'outer'), None, 'head'), may hold values from -32 to 32
- offsets: int32 [16, 2], replicated, may hold values from 0 to 1984, as said below
Outputs:
- grad_query: bfloat16 [16, 128, 4096], P(('inner', 'outer'), 'head')
- grad_key: bfloat16 [16, 128, 512], P(('inner', 'outer'), 'head')
- grad_value: bfloat16 [16, 128, 512], P(('inner', 'outer'), 'head')
Inputs may be any that keep to these rules, and one draw needn't show every extreme that they name: `offsets`: row b holds p * 64 and (31 - p) * 64, where p runs over a permutation of 0 to 15, so that all blocks' positions together are 0 to 2047, each once.
All inputs are finite; a program needn't handle non-finite values.
Results may differ from a plain program's by a relative error of at most 0.0058.
Values may be sent and summed in bfloat16 or wider, within the bound.
No kernel may reach another device: no remote copies, remote signals or barrier semaphores. Data moves between devices by JAX's collectives and lax.ppermute only.
A program may use at most 64 MiB of HBM per device.

v0:
```python
import math

import jax
import jax.numpy as jnp
from jax import lax
from jax.sharding import PartitionSpec as P

HEAD_WIDTH = 128
QUERY_HEADS = 32
KEY_VALUE_HEADS = 4
INNER_STEPS = 3
OUTER_STEPS = 2


def shifted(value, axis, steps):
    count = lax.axis_size(axis)
    pairs = [(source, (source + steps) % count) for source in range(count)]
    return lax.ppermute(value, axis, pairs)


def shift_pairs_inner(stacked, stride):
    return shifted(stacked, "inner", stride)


def shift_pairs_outer(stacked, stride):
    return shifted(stacked, "outer", stride)


def shift_sums_inner(stacked, stride):
    return shifted(stacked, "inner", stride)


def shift_sums_outer(stacked, stride):
    return shifted(stacked, "outer", stride)


def local_positions(offsets, block_index, tokens_per_block):
    halfway = tokens_per_block // 2
    within = jnp.arange(tokens_per_block, dtype=jnp.int32)
    offset_row = lax.dynamic_index_in_dim(offsets, block_index, 0, keepdims=False)
    return jnp.where(within < halfway, offset_row[0], offset_row[1]) + within % halfway


def visit_order():
    visits = []
    for outer_step in range(OUTER_STEPS):
        sweep_order = list(range(INNER_STEPS))
        if outer_step % 2 == 1:
            sweep_order = sweep_order[::-1]
        visits = visits + [(inner_step, outer_step) for inner_step in sweep_order]
    return visits


def pair_terms(
    query_heads, grad_heads, norm_heads, dot_heads, query_pos, key_heads, value_heads, key_pos
):
    scaling = 1.0 / math.sqrt(HEAD_WIDTH)
    scores = (
        jnp.einsum("tgjd,ugd->gjtu", query_heads, key_heads, preferred_element_type=jnp.float32)
        * scaling
    )
    visible = key_pos[None, :] <= query_pos[:, None]
    probabilities = jnp.where(visible, jnp.exp(scores - norm_heads[..., None]), 0.0)
    grad_probs = jnp.einsum(
        "tgjd,ugd->gjtu", grad_heads, value_heads, preferred_element_type=jnp.float32
    )
    grad_scores = probabilities * (grad_probs - dot_heads[..., None])
    probs_low = probabilities.astype(jnp.bfloat16)
    scores_low = grad_scores.astype(jnp.bfloat16)
    grad_value = jnp.einsum(
        "gjtu,tgjd->ugd", probs_low, grad_heads, preferred_element_type=jnp.float32
    )
    grad_key = scaling * jnp.einsum(
        "gjtu,tgjd->ugd", scores_low, query_heads, preferred_element_type=jnp.float32
    )
    grad_query = scaling * jnp.einsum(
        "gjtu,ugd->tgjd", scores_low, key_heads, preferred_element_type=jnp.float32
    )
    tokens_per_block = query_heads.shape[0]
    key_rows = key_heads.shape[0]
    return (
        grad_query.reshape(tokens_per_block, -1),
        grad_key.reshape(key_rows, -1),
        grad_value.reshape(key_rows, -1),
    )


def shards(queries, keys, values, grad_out, log_denominator, output_row_dot, offsets):
    tokens_per_block = queries.shape[1]
    query_cols = queries.shape[2]
    key_value_columns = keys.shape[2]
    heads_kv = key_value_columns // HEAD_WIDTH
    heads_per_group = QUERY_HEADS // KEY_VALUE_HEADS
    query_heads = queries.reshape(tokens_per_block, heads_kv, heads_per_group, HEAD_WIDTH)
    grad_heads = grad_out.reshape(tokens_per_block, heads_kv, heads_per_group, HEAD_WIDTH)
    norm_heads = jnp.transpose(
        log_denominator.reshape(tokens_per_block, heads_kv, heads_per_group), (1, 2, 0)
    )
    dot_heads = jnp.transpose(
        output_row_dot.reshape(tokens_per_block, heads_kv, heads_per_group), (1, 2, 0)
    )
    inner_count = lax.axis_size("inner")
    outer_count = lax.axis_size("outer")
    inner_here = lax.axis_index("inner")
    outer_here = lax.axis_index("outer")
    query_pos = local_positions(offsets, inner_here * outer_count + outer_here, tokens_per_block)
    held_pair = jnp.stack([keys[0], values[0]])
    key_sums = jnp.zeros((2, tokens_per_block, key_value_columns), jnp.float32)
    grad_query = jnp.zeros((tokens_per_block, query_cols), jnp.float32)
    visits = visit_order()
    previous = (0, 0)
    for inner_step, outer_step in visits:
        if inner_step != previous[0]:
            held_pair = shift_pairs_inner(held_pair, inner_step - previous[0])
            key_sums = shift_sums_inner(key_sums, inner_step - previous[0])
        elif outer_step != previous[1]:
            held_pair = shift_pairs_outer(held_pair, outer_step - previous[1])
            key_sums = shift_sums_outer(key_sums, outer_step - previous[1])
        previous = (inner_step, outer_step)
        source = jnp.mod(inner_here - inner_step, inner_count) * outer_count + jnp.mod(
            outer_here - outer_step, outer_count
        )
        key_pos = local_positions(offsets, source, tokens_per_block)
        key_heads = held_pair[0].reshape(tokens_per_block, heads_kv, HEAD_WIDTH)
        value_heads = held_pair[1].reshape(tokens_per_block, heads_kv, HEAD_WIDTH)
        term_query, term_key, term_value = pair_terms(
            query_heads,
            grad_heads,
            norm_heads,
            dot_heads,
            query_pos,
            key_heads,
            value_heads,
            key_pos,
        )
        grad_query = grad_query + term_query
        key_sums = key_sums + jnp.stack([term_key, term_value])
    key_sums = shift_sums_outer(key_sums, -previous[1])
    query_done, key_done, value_done = (
        lax.all_to_all(
            grad_query.astype(jnp.bfloat16), "head", split_axis=0, concat_axis=1, tiled=True
        ),
        lax.all_to_all(
            key_sums[0].astype(jnp.bfloat16), "head", split_axis=0, concat_axis=1, tiled=True
        ),
        lax.all_to_all(
            key_sums[1].astype(jnp.bfloat16), "head", split_axis=0, concat_axis=1, tiled=True
        ),
    )
    return (
        query_done.reshape(1, query_done.shape[0], query_done.shape[1]),
        key_done.reshape(1, key_done.shape[0], key_done.shape[1]),
        value_done.reshape(1, value_done.shape[0], value_done.shape[1]),
    )


def solution(mesh):
    return jax.shard_map(
        shards,
        mesh=mesh,
        in_specs=(
            P(("inner", "outer"), None, "head"),
            P(("inner", "outer"), None, "head"),
            P(("inner", "outer"), None, "head"),
            P(("inner", "outer"), None, "head"),
            P(("inner", "outer"), None, "head"),
            P(("inner", "outer"), None, "head"),
            P(),
        ),
        out_specs=(
            P(("inner", "outer"), "head", None),
            P(("inner", "outer"), "head", None),
            P(("inner", "outer"), "head", None),
        ),
        check_vma=False,
    )
```

profile of v0, /device:TPU:0, one launch (start us, length us, event | category | flops | bytes accessed | tf_op | source)
XLA Modules:
  0.0 101.5 jit_solution(13334101803015794710)
XLA Ops:
  0.7 0.7 copy-done.5
  1.5 0.6 fusion.86
  2.1 0.6 fusion.84
  2.6 0.5 fusion.83
  3.2 0.5 fusion.82
  3.7 0.6 fusion.81
  4.3 0.5 fusion.85
  4.8 0.5 fusion.87
  5.3 1.4 %copy.299 = bf16[1,128,2048]{1,2,0:T(8,128)(2,1)S(1)} copy(bf16[1,128,2048]{2,1,0:T(8,128)(2,1)} %param.7) | data formatting | bytes 1048576 | tf_op jit(solution)/shard_map/reshape | solution.py:94
  7.1 0.6 copy-done.4
  7.6 1.2 %select_add_fusion.6 = s32[128]{0:T(128)S(1)} fusion(s32[]{:T(128)} %bitcast.1, s32[]{:T(128)} %bitcast), kind=kLoop, calls=%fused_computation.126 | loop fusion | flops 1152 | bytes 520 | tf_op jit(solution)/shard_map/add | solution.py:41
  8.8 2.5 %select_add_fusion.2 = (s32[128]{0:T(128)S(1)}, s32[128]{0:T(128)S(1)}) fusion(s32[]{:T(128)} %bitcast.40, s32[]{:T(128)} %bitcast.39, s32[]{:T(128)} %bitcast.29, s32[]{:T(128)} %bitcast.28), kind=kLoop, calls=%fused_computation.122 | loop fusion | flops 1408 | bytes 1040 | tf_op jit(solution)/shard_map/add | solution.py:41
  11.3 2.5 %select_add_fusion = (s32[128]{0:T(128)S(1)}, s32[128]{0:T(128)S(1)}) fusion(s32[]{:T(128)} %bitcast.62, s32[]{:T(128)} %bitcast.61, s32[]{:T(128)} %bitcast.51, s32[]{:T(128)} %bitcast.50), kind=kLoop, calls=%fused_computation.120 | loop fusion | flops 1408 | bytes 1040 | tf_op jit(solution)/shard_map/add | solution.py:41
  13.8 2.5 %select_add_fusion.4 = (s32[128]{0:T(128)S(1)}, s32[128]{0:T(128)S(1)}) fusion(s32[]{:T(128)} %bitcast.18, s32[]{:T(128)} %bitcast.17, s32[]{:T(128)} %bitcast.3, s32[]{:T(128)} %bitcast.2), kind=kLoop, calls=%fused_computation.124 | loop fusion | flops 1408 | bytes 1040 | tf_op jit(solution)/shard_map/add | solution.py:41
  18.8 0.7 pad_maximum_fusion
  20.3 2.6 %collective-permute-start = (bf16[2,128,256]{1,2,0:T(8,128)(2,1)S(1)}, bf16[2,128,256]{1,2,0:T(8,128)(2,1)S(1)}, u32[]{:S(2)}, u32[]{:S(2)}) collective-permute-start(bf16[2,128,256]{1,2,0:T(8,128)(2,1)S(1)} %pad_maximum_fusion.1), channel_id=1, source_target_pairs={{0,4},{4,8},{8,12},{12,0},{1,5},{5,9},{9,13},{13,1},{2,6},{6,10},{... | collective-permute-start | bytes 393224 | tf_op jit(solution)/shard_map/ppermute | solution.py:18
  23.3 4.3 %collective-permute-done = bf16[2,128,256]{1,2,0:T(8,128)(2,1)S(1)} collective-permute-done((bf16[2,128,256]{1,2,0:T(8,128)(2,1)S(1)}, bf16[2,128,256]{1,2,0:T(8,128)(2,1)S(1)}, u32[]{:S(2)}, u32[]{:S(2)}) %collective-permute-start) | collective-permute-done | bytes 131104 | tf_op jit(solution)/shard_map/ppermute | solution.py:18
  29.6 0.7 maximum_add_fusion
  30.4 2.4 %collective-permute-start.6 = (f32[2,128,256]{2,1,0:T(8,128)}, f32[2,128,256]{2,1,0:T(8,128)}, u32[]{:S(2)}, u32[]{:S(2)}) collective-permute-start(f32[2,128,256]{2,1,0:T(8,128)} %maximum_add_fusion), channel_id=1, source_target_pairs={{0,4},{4,8},{8,12},{12,0},{1,5},{5,9},{9,13},{13,1},{2,6},{6,10},{... | collective-permute-start | bytes 786440 | tf_op jit(solution)/shard_map/ppermute | solution.py:18
  32.8 1.0 collective-permute-done.1
  33.7 0.9 fusion.79
  36.0 2.4 %collective-permute-start.2 = (bf16[2,128,256]{1,2,0:T(8,128)(2,1)}, bf16[2,128,256]{1,2,0:T(8,128)(2,1)S(1)}, u32[]{:S(2)}, u32[]{:S(2)}) collective-permute-start(bf16[2,128,256]{1,2,0:T(8,128)(2,1)} %collective-permute-done.1), channel_id=1, source_target_pairs={{0,1},{1,2},{2,3},{3,0},{4,5},{5,6},{6,7},{7,4},{8,9},{9,10},{10,1... | collective-permute-start | bytes 393224 | tf_op jit(solution)/shard_map/ppermute | solution.py:18
  39.0 4.7 %collective-permute-done.2 = bf16[2,128,256]{1,2,0:T(8,128)(2,1)S(1)} collective-permute-done((bf16[2,128,256]{1,2,0:T(8,128)(2,1)}, bf16[2,128,256]{1,2,0:T(8,128)(2,1)S(1)}, u32[]{:S(2)}, u32[]{:S(2)}) %collective-permute-start.2) | collective-permute-done | bytes 131104 | tf_op jit(solution)/shard_map/ppermute | solution.py:18
  45.7 1.0 maximum_add_fusion.1
  46.7 1.1 %collective-permute-done.3 = bf16[2,128,256]{1,2,0:T(8,128)(2,1)S(1)} collective-permute-done((bf16[2,128,256]{1,2,0:T(8,128)(2,1)S(1)}, bf16[2,128,256]{1,2,0:T(8,128)(2,1)S(1)}, u32[]{:S(2)}, u32[]{:S(2)}) %collective-permute-start.3) | collective-permute-done | bytes 131104 | tf_op jit(solution)/shard_map/ppermute | solution.py:18
  48.9 1.3 %fusion.19 = f32[128,2,8,128]{3,0,2,1:T(8,128)} fusion(f32[128,2,8,128]{3,0,2,1:T(8,128)S(1)} %fusion.25, bf16[128,2,128,1]{0,2,3,1:T(8,128)(2,1)S(1)} %bitcast.388, bf16[2,8,128,128]{2,3,1,0:T(8,128)(2,1)S(1)} %fusion.49), kind=kOutput, calls=%fused_computation.28 | convolution fusion | flops 67633152 | bytes 2686976 | tf_op jit(solution)/shard_map/gjtu,ugd->tgjd/dot_general | solution.py:76
  50.2 1.9 %collective-permute-start.4 = (bf16[2,128,256]{1,2,0:T(8,128)(2,1)S(1)}, bf16[2,128,256]{1,2,0:T(8,128)(2,1)S(1)}, u32[]{:S(2)}, u32[]{:S(2)}) collective-permute-start(bf16[2,128,256]{1,2,0:T(8,128)(2,1)S(1)} %collective-permute-done.3), channel_id=1, source_target_pairs={{0,12},{4,0},{8,4},{12,8},{1,13},{5,1},{9,5},{13,9},{2,14},{6,2},{... | collective-permute-start | bytes 393224 | tf_op jit(solution)/shard_map/ppermute | solution.py:18
  52.6 2.0 %collective-permute-done.4 = bf16[2,128,256]{1,2,0:T(8,128)(2,1)S(1)} collective-permute-done((bf16[2,128,256]{1,2,0:T(8,128)(2,1)S(1)}, bf16[2,128,256]{1,2,0:T(8,128)(2,1)S(1)}, u32[]{:S(2)}, u32[]{:S(2)}) %collective-permute-start.4) | collective-permute-done | bytes 131104 | tf_op jit(solution)/shard_map/ppermute | solution.py:18
  55.0 2.2 %collective-permute-done.7 = f32[2,128,256]{2,1,0:T(8,128)S(1)} collective-permute-done((f32[2,128,256]{2,1,0:T(8,128)S(1)}, f32[2,128,256]{2,1,0:T(8,128)S(1)}, u32[]{:S(2)}, u32[]{:S(2)}) %collective-permute-start.7) | collective-permute-done | bytes 262176 | tf_op jit(solution)/shard_map/ppermute | solution.py:18
  57.2 0.7 maximum_add_fusion.2
  58.0 0.9 collective-permute-start.8
  59.7 3.4 %collective-permute-done.8 = f32[2,128,256]{2,1,0:T(8,128)} collective-permute-done((f32[2,128,256]{2,1,0:T(8,128)}, f32[2,128,256]{2,1,0:T(8,128)}, u32[]{:S(2)}, u32[]{:S(2)}) %collective-permute-start.8) | collective-permute-done | bytes 262176 | tf_op jit(solution)/shard_map/ppermute | solution.py:18
  63.1 1.0 maximum_add_fusion.3
  64.1 2.0 %collective-permute-start.9 = (f32[2,128,256]{2,1,0:T(8,128)S(1)}, f32[2,128,256]{2,1,0:T(8,128)S(1)}, u32[]{:S(2)}, u32[]{:S(2)}) collective-permute-start(f32[2,128,256]{2,1,0:T(8,128)S(1)} %maximum_add_fusion.3), channel_id=1, source_target_pairs={{0,12},{4,0},{8,4},{12,8},{1,13},{5,1},{9,5},{13,9},{2,14},{6,2},{... | collective-permute-start | bytes 786440 | tf_op jit(solution)/shard_map/ppermute | solution.py:18
  66.5 3.5 %collective-permute-done.9 = f32[2,128,256]{2,1,0:T(8,128)S(1)} collective-permute-done((f32[2,128,256]{2,1,0:T(8,128)S(1)}, f32[2,128,256]{2,1,0:T(8,128)S(1)}, u32[]{:S(2)}, u32[]{:S(2)}) %collective-permute-start.9) | collective-permute-done | bytes 262176 | tf_op jit(solution)/shard_map/ppermute | solution.py:18
  70.0 1.2 %collective-permute-start.10 = (bf16[2,128,256]{2,1,0:T(8,128)(2,1)S(1)}, bf16[2,128,256]{2,1,0:T(8,128)(2,1)S(1)}, u32[]{:S(2)}, u32[]{:S(2)}) collective-permute-start(bf16[2,128,256]{2,1,0:T(8,128)(2,1)S(1)} %maximum_add_fusion.4), channel_id=1, source_target_pairs={{0,3},{1,0},{2,1},{3,2},{4,7},{5,4},{6,5},{7,6},{8,11},{9,8},{10,9... | collective-permute-start | bytes 393224 | tf_op jit(solution)/shard_map/ppermute | solution.py:18
  71.2 1.6 %fusion.47 = bf16[128,2,8,128]{3,0,2,1:T(8,128)(2,1)S(1)} fusion(f32[128,2,8,128]{3,0,2,1:T(8,128)} %fusion.19, bf16[128,2,128,1]{0,2,3,1:T(8,128)(2,1)S(1)} %bitcast.380, bf16[2,8,128,128]{2,3,1,0:T(8,128)(2,1)S(1)} %fusion.48), kind=kOutput, calls=%fused_computation.65 | convolution fusion | flops 67895296 | bytes 2162688 | tf_op jit(solution)/shard_map/gjtu,ugd->tgjd/dot_general | solution.py:76
  73.1 1.0 %reshape.148 = bf16[2,64,2048]{2,1,0:T(8,128)(2,1)} reshape(bf16[128,2,8,128]{3,2,1,0:T(8,128)(2,1)S(1)} %copy.180) | data formatting | bytes 1048576 | tf_op jit(solution)/shard_map/convert_element_type | solution.py:141
  74.1 3.5 %all-to-all-start = ((bf16[2,64,2048]{2,1,0:T(8,128)(2,1)}), bf16[2,64,2048]{2,1,0:T(8,128)(2,1)S(1)}, u32[]{:S(2)}, u32[]{:S(2)}) async-start(bf16[2,64,2048]{2,1,0:T(8,128)(2,1)} %reshape.148), calls=%async_computation | async-start | bytes 1048576 | tf_op jit(solution)/shard_map/all_to_all | solution.py:140
  77.6 0.6 fusion.75
  78.3 8.6 %all-to-all-done = bf16[2,64,2048]{2,1,0:T(8,128)(2,1)S(1)} async-done(((bf16[2,64,2048]{2,1,0:T(8,128)(2,1)}), bf16[2,64,2048]{2,1,0:T(8,128)(2,1)S(1)}, u32[]{:S(2)}, u32[]{:S(2)}) %all-to-all-start) | async-done | bytes 524320 | tf_op jit(solution)/shard_map/all_to_all | solution.py:140
  86.8 6.5 %all_to_all.39 = bf16[2,64,256]{2,1,0:T(8,128)(2,1)S(1)} all-to-all(bf16[2,64,256]{2,1,0:T(8,128)(2,1)S(1)} %bitcast.421), channel_id=1, replica_groups=mesh['head'=2,'inner'=4,'outer'=4] {'head'}, dimensions={0} | all-to-all | bytes 131072 | tf_op jit(solution)/shard_map/all_to_all | solution.py:143
  93.3 3.3 %all-to-all-start.2 = ((bf16[2,64,256]{2,1,0:T(8,128)(2,1)}), bf16[2,64,256]{2,1,0:T(8,128)(2,1)S(1)}, u32[]{:S(2)}, u32[]{:S(2)}) async-start(bf16[2,64,256]{2,1,0:T(8,128)(2,1)} %bitcast.120), calls=%async_computation.2 | async-start | bytes 131072 | tf_op jit(solution)/shard_map/all_to_all | solution.py:146
  96.6 0.5 copy.181
  97.2 1.2 %reshape.142 = bf16[1,64,4096]{2,1,0:T(8,128)(2,1)} reshape(bf16[64,2,2048]{2,1,0:T(2,128)(2,1)S(1)} %copy.181) | data formatting | bytes 1048576 | tf_op jit(solution)/shard_map/reshape | solution.py:151
  98.4 0.7 reshape.143
  99.1 1.6 %all-to-all-done.2 = bf16[2,64,256]{2,1,0:T(8,128)(2,1)S(1)} async-done(((bf16[2,64,256]{2,1,0:T(8,128)(2,1)}), bf16[2,64,256]{2,1,0:T(8,128)(2,1)S(1)}, u32[]{:S(2)}, u32[]{:S(2)}) %all-to-all-start.2) | async-done | bytes 65568 | tf_op jit(solution)/shard_map/all_to_all | solution.py:146
  100.8 0.7 reshape.144
  (73 shorter events, 13.4 us)
Async XLA Ops:
  0.7 0.7 copy-start.5
  5.3 1.4 %copy-start.3 = (bf16[1,128,256]{2,1,0:T(8,128)(2,1)S(1)}, bf16[1,128,256]{2,1,0:T(8,128)(2,1)}, u32[]{:S(2)}) copy-start(bf16[1,128,256]{2,1,0:T(8,128)(2,1)} %param.8) | copy-start | bytes 196612
  5.3 1.4 %copy-start = (bf16[1,128,2048]{2,1,0:T(8,128)(2,1)S(1)}, bf16[1,128,2048]{2,1,0:T(8,128)(2,1)}, u32[]{:S(2)}) copy-start(bf16[1,128,2048]{2,1,0:T(8,128)(2,1)} %param.10) | copy-start | bytes 1572868
  6.8 0.8 copy-start.4
  16.3 0.7 copy-start.1
  17.3 0.7 copy-start.2
  19.5 10.1 %collective-permute-start.5 = (f32[2,128,256]{2,1,0:T(8,128)}, f32[2,128,256]{2,1,0:T(8,128)S(1)}, u32[]{:S(2)}, u32[]{:S(2)}) collective-permute-start(f32[2,128,256]{2,1,0:T(8,128)} %pad_maximum_fusion), channel_id=1, source_target_pairs={{0,4},{4,8},{8,12},{12,0},{1,5},{5,9},{9,13},{13,1},{2,6},{6,10},{... | collective-permute-start | bytes 786440 | tf_op jit(solution)/shard_map/ppermute | solution.py:18
  20.3 7.3 %collective-permute-start = (bf16[2,128,256]{1,2,0:T(8,128)(2,1)S(1)}, bf16[2,128,256]{1,2,0:T(8,128)(2,1)S(1)}, u32[]{:S(2)}, u32[]{:S(2)}) collective-permute-start(bf16[2,128,256]{1,2,0:T(8,128)(2,1)S(1)} %pad_maximum_fusion.1), channel_id=1, source_target_pairs={{0,4},{4,8},{8,12},{12,0},{1,5},{5,9},{9,13},{13,1},{2,6},{6,10},{... | collective-permute-start | bytes 393224 | tf_op jit(solution)/shard_map/ppermute | solution.py:18
  29.2 4.5 %collective-permute-start.1 = (bf16[2,128,256]{1,2,0:T(8,128)(2,1)S(1)}, bf16[2,128,256]{1,2,0:T(8,128)(2,1)}, u32[]{:S(2)}, u32[]{:S(2)}) collective-permute-start(bf16[2,128,256]{1,2,0:T(8,128)(2,1)S(1)} %collective-permute-done), channel_id=1, source_target_pairs={{0,4},{4,8},{8,12},{12,0},{1,5},{5,9},{9,13},{13,1},{2,6},{6,10},{... | collective-permute-start | bytes 393224 | tf_op jit(solution)/shard_map/ppermute | solution.py:18
  30.4 15.3 %collective-permute-start.6 = (f32[2,128,256]{2,1,0:T(8,128)}, f32[2,128,256]{2,1,0:T(8,128)}, u32[]{:S(2)}, u32[]{:S(2)}) collective-permute-start(f32[2,128,256]{2,1,0:T(8,128)} %maximum_add_fusion), channel_id=1, source_target_pairs={{0,4},{4,8},{8,12},{12,0},{1,5},{5,9},{9,13},{13,1},{2,6},{6,10},{... | collective-permute-start | bytes 786440 | tf_op jit(solution)/shard_map/ppermute | solution.py:18
  36.0 7.6 %collective-permute-start.2 = (bf16[2,128,256]{1,2,0:T(8,128)(2,1)}, bf16[2,128,256]{1,2,0:T(8,128)(2,1)S(1)}, u32[]{:S(2)}, u32[]{:S(2)}) collective-permute-start(bf16[2,128,256]{1,2,0:T(8,128)(2,1)} %collective-permute-done.1), channel_id=1, source_target_pairs={{0,1},{1,2},{2,3},{3,0},{4,5},{5,6},{6,7},{7,4},{8,9},{9,10},{10,1... | collective-permute-start | bytes 393224 | tf_op jit(solution)/shard_map/ppermute | solution.py:18
  45.3 2.6 %collective-permute-start.3 = (bf16[2,128,256]{1,2,0:T(8,128)(2,1)S(1)}, bf16[2,128,256]{1,2,0:T(8,128)(2,1)S(1)}, u32[]{:S(2)}, u32[]{:S(2)}) collective-permute-start(bf16[2,128,256]{1,2,0:T(8,128)(2,1)S(1)} %collective-permute-done.2), channel_id=1, source_target_pairs={{0,12},{4,0},{8,4},{12,8},{1,13},{5,1},{9,5},{13,9},{2,14},{6,2},{... | collective-permute-start | bytes 393224 | tf_op jit(solution)/shard_map/ppermute | solution.py:18
  46.7 10.6 %collective-permute-start.7 = (f32[2,128,256]{2,1,0:T(8,128)S(1)}, f32[2,128,256]{2,1,0:T(8,128)S(1)}, u32[]{:S(2)}, u32[]{:S(2)}) collective-permute-start(f32[2,128,256]{2,1,0:T(8,128)S(1)} %maximum_add_fusion.1), channel_id=1, source_target_pairs={{0,1},{1,2},{2,3},{3,0},{4,5},{5,6},{6,7},{7,4},{8,9},{9,10},{10,1... | collective-permute-start | bytes 786440 | tf_op jit(solution)/shard_map/ppermute | solution.py:18
  50.2 4.4 %collective-permute-start.4 = (bf16[2,128,256]{1,2,0:T(8,128)(2,1)S(1)}, bf16[2,128,256]{1,2,0:T(8,128)(2,1)S(1)}, u32[]{:S(2)}, u32[]{:S(2)}) collective-permute-start(bf16[2,128,256]{1,2,0:T(8,128)(2,1)S(1)} %collective-permute-done.3), channel_id=1, source_target_pairs={{0,12},{4,0},{8,4},{12,8},{1,13},{5,1},{9,5},{13,9},{2,14},{6,2},{... | collective-permute-start | bytes 393224 | tf_op jit(solution)/shard_map/ppermute | solution.py:18
  58.0 5.2 %collective-permute-start.8 = (f32[2,128,256]{2,1,0:T(8,128)}, f32[2,128,256]{2,1,0:T(8,128)}, u32[]{:S(2)}, u32[]{:S(2)}) collective-permute-start(f32[2,128,256]{2,1,0:T(8,128)} %maximum_add_fusion.2), channel_id=1, source_target_pairs={{0,12},{4,0},{8,4},{12,8},{1,13},{5,1},{9,5},{13,9},{2,14},{6,2},{... | collective-permute-start | bytes 786440 | tf_op jit(solution)/shard_map/ppermute | solution.py:18
  64.1 5.8 %collective-permute-start.9 = (f32[2,128,256]{2,1,0:T(8,128)S(1)}, f32[2,128,256]{2,1,0:T(8,128)S(1)}, u32[]{:S(2)}, u32[]{:S(2)}) collective-permute-start(f32[2,128,256]{2,1,0:T(8,128)S(1)} %maximum_add_fusion.3), channel_id=1, source_target_pairs={{0,12},{4,0},{8,4},{12,8},{1,13},{5,1},{9,5},{13,9},{2,14},{6,2},{... | collective-permute-start | bytes 786440 | tf_op jit(solution)/shard_map/ppermute | solution.py:18
  70.0 7.6 %collective-permute-start.10 = (bf16[2,128,256]{2,1,0:T(8,128)(2,1)S(1)}, bf16[2,128,256]{2,1,0:T(8,128)(2,1)S(1)}, u32[]{:S(2)}, u32[]{:S(2)}) collective-permute-start(bf16[2,128,256]{2,1,0:T(8,128)(2,1)S(1)} %maximum_add_fusion.4), channel_id=1, source_target_pairs={{0,3},{1,0},{2,1},{3,2},{4,7},{5,4},{6,5},{7,6},{8,11},{9,8},{10,9... | collective-permute-start | bytes 393224 | tf_op jit(solution)/shard_map/ppermute | solution.py:18
  74.1 12.7 %all-to-all-start = ((bf16[2,64,2048]{2,1,0:T(8,128)(2,1)}), bf16[2,64,2048]{2,1,0:T(8,128)(2,1)S(1)}, u32[]{:S(2)}, u32[]{:S(2)}) async-start(bf16[2,64,2048]{2,1,0:T(8,128)(2,1)} %reshape.148), calls=%async_computation | async-start | bytes 1048576 | tf_op jit(solution)/shard_map/all_to_all | solution.py:140
  93.3 7.4 %all-to-all-start.2 = ((bf16[2,64,256]{2,1,0:T(8,128)(2,1)}), bf16[2,64,256]{2,1,0:T(8,128)(2,1)S(1)}, u32[]{:S(2)}, u32[]{:S(2)}) async-start(bf16[2,64,256]{2,1,0:T(8,128)(2,1)} %bitcast.120), calls=%async_computation.2 | async-start | bytes 131072 | tf_op jit(solution)/shard_map/all_to_all | solution.py:146
where the time goes:
time: 102 us; the launch traced here: 101 us
  waiting for transfers between devices  32.4 us (32%)
  starting transfers between devices  20.9 us (20%)
  local copies, waits for them, and re-layouts  15.3 us (15%)
  other arithmetic  13 us (13%)
  matrix products  12.2 us (12%)
  blocking collectives  6.49 us (6%)
  between operations  1.3 us (1%)
    ppermute x11, waiting for transfers between devices, shifted(): return lax.ppermute(value, axis, pairs)  22.2 us
    ppermute x11, starting transfers between devices, shifted(): return lax.ppermute(value, axis, pairs)  14.1 us
    add x4, other arithmetic, local_positions(): jnp.where(within < halfway, offset_row[0], offset_row[1]) + within % halfway  8.61 us
    all_to_all x1, waiting for transfers between devices, shards(): lax.all_to_all(grad_query.astype(jnp.bfloat16), 'head', split_axis=0, con...  8.56 us
    all_to_all x1, blocking collectives, shards(): lax.all_to_all(key_sums[0].astype(jnp.bfloat16), 'head', split_axis=0, co...  6.49 us
    dot_general x6, matrix products, pair_terms(): jnp.einsum('gjtu,ugd->tgjd', scores_low, key_heads, preferred_element_typ...  4.3 us
    slice x7, local copies, waits for them, and re-layouts, local_positions(): offset_row[0]  3.85 us
    all_to_all x1, starting transfers between devices, shards(): lax.all_to_all(grad_query.astype(jnp.bfloat16), 'head', split_axis=0, con...  3.49 us
  transfers between devices with their start and end apart: 13, of which 10 were waited for; matrix products, arithmetic and copies ran while one was open for 19% of the time, Pallas kernels for 0%

commit v1 on v0

v1 whole, which is shorter than its diff:
```python
import math

import jax
import jax.numpy as jnp
from jax import lax
from jax.experimental import pallas as pl
from jax.experimental.pallas import tpu as pltpu
from jax.sharding import PartitionSpec as P

HEAD_WIDTH = 128
QUERY_HEADS = 32
KEY_VALUE_HEADS = 4
FAR = 2
BACK = 1

SCALE = 1.0 / math.sqrt(HEAD_WIDTH)
VMEM = pl.BlockSpec(memory_space=pltpu.VMEM)
SMEM = pl.BlockSpec(memory_space=pltpu.SMEM)
F32 = jnp.float32
BF16 = jnp.bfloat16
VMEM_LIMIT = 24 * 1024 * 1024


def dot_nt(a, b):
    return lax.dot_general(a, b, (((1,), (1,)), ((), ())), preferred_element_type=F32)


def dot_nn(a, b):
    return lax.dot_general(a, b, (((1,), (0,)), ((), ())), preferred_element_type=F32)


def call(kernel, name, out_shape, in_specs, *, flops=0, bytes_accessed=0, aliases=None, scratch=()):
    return pl.pallas_call(
        kernel,
        name=name,
        out_shape=out_shape,
        in_specs=in_specs,
        out_specs=jax.tree.map(lambda _: VMEM, out_shape),
        scratch_shapes=scratch,
        input_output_aliases=aliases or {},
        cost_estimate=pl.CostEstimate(flops=flops, bytes_accessed=bytes_accessed, transcendentals=0),
        compiler_params=pltpu.CompilerParams(vmem_limit_bytes=VMEM_LIMIT),
    )


def prep_kernel(k_ref, v_ref, norm_ref, dot_ref, kv_ref, rows_ref):
    kv_ref[0] = k_ref[...]
    kv_ref[1] = v_ref[...]
    tokens = norm_ref.shape[1]
    half = tokens // 2
    pairs = norm_ref.shape[0] // 2
    lanes = lax.broadcasted_iota(jnp.int32, (pairs, tokens), 1)
    for at, ref in enumerate((norm_ref, dot_ref)):
        even = ref[pl.ds(0, pairs, stride=2), :]
        odd = ref[pl.ds(1, pairs, stride=2), :]
        rows_ref[at, 0] = jnp.where(lanes < half, even, pltpu.roll(odd, half, 1))
        rows_ref[at, 1] = jnp.where(lanes < half, pltpu.roll(even, half, 1), odd)


def quadrant(query, kv_ref, slot, key_half, query_half, diagonal, first, sums_ref):
    q_ref, do_ref, rows_ref, dq_ref = query
    tokens = q_ref.shape[0]
    half = tokens // 2
    heads_kv = kv_ref.shape[-1] // HEAD_WIDTH
    per_group = q_ref.shape[1] // HEAD_WIDTH // heads_kv
    chunk = 4
    def rows_of(which):
        if isinstance(which, int):
            return pl.ds(which * half, half)
        return pl.ds(pl.multiple_of(which * half, half), half)

    key_rows, query_rows = rows_of(key_half), rows_of(query_half)
    if diagonal:
        u = lax.broadcasted_iota(jnp.int32, (half, chunk * half), 0)
        t = lax.broadcasted_iota(jnp.int32, (half, chunk * half), 1) % half
        visible = u <= t
    for g in range(heads_kv):
        cols = slice(g * HEAD_WIDTH, (g + 1) * HEAD_WIDTH)
        k = kv_ref[0, key_rows, cols]
        v = kv_ref[1, key_rows, cols]
        kt = k.T
        dk = dv = None
        for c in range(per_group // chunk):
            heads = [g * per_group + c * chunk + j for j in range(chunk)]
            qc = jnp.concatenate([q_ref[query_rows, h * HEAD_WIDTH : (h + 1) * HEAD_WIDTH] for h in heads], 0)
            doc = jnp.concatenate([do_ref[query_rows, h * HEAD_WIDTH : (h + 1) * HEAD_WIDTH] for h in heads], 0)
            pair = heads[0] // 2
            norm = jnp.concatenate([rows_ref[0, query_half, pl.ds(pair + i, 1), :] for i in range(chunk // 2)], 1)
            dots = jnp.concatenate([rows_ref[1, query_half, pl.ds(pair + i, 1), :] for i in range(chunk // 2)], 1)
            prob = jnp.exp(dot_nt(k, qc) * SCALE - norm)
            if diagonal:
                prob = jnp.where(visible, prob, 0.0)
            grad = prob * (dot_nt(v, doc) - dots)
            prob_low = prob.astype(BF16)
            grad_low = grad.astype(BF16)
            dv_c = dot_nn(prob_low, doc)
            dk_c = dot_nn(grad_low, qc)
            dv = dv_c if dv is None else dv + dv_c
            dk = dk_c if dk is None else dk + dk_c
            dq = dot_nn(kt, grad_low)
            for i in range(chunk // 2):
                part = dq[:, i * tokens : (i + 1) * tokens]
                if first:
                    dq_ref[query_half, pair + i] = part
                else:
                    dq_ref[query_half, pair + i] += part
        sums_ref[slot, 0, key_rows, cols] += dk
        sums_ref[slot, 1, key_rows, cols] += dv


def wrapped(index, steps, count):
    moved = index - steps
    return jnp.where(moved < 0, moved + count, moved)


def visit(off_ref, mine, other, kv_ref, sums_ref, slot, inner_back, outer_back, own):
    inner_count, outer_count = lax.axis_size("inner"), lax.axis_size("outer")
    i, o = lax.axis_index("inner"), lax.axis_index("outer")
    odd = i & 1
    key_block = wrapped(i, inner_back, inner_count) * outer_count + wrapped(o, outer_back, outer_count)
    key_start = off_ref[key_block, 0]

    def full(query, block, first):
        which = jnp.where(key_start < off_ref[block, 0], 0, 1)
        quadrant(query, kv_ref, slot, 0, 1, False, first, sums_ref)
        quadrant(query, kv_ref, slot, which, which, False, False, sums_ref)

    if own:
        quadrant(mine, kv_ref, slot, 0, 1, False, True, sums_ref)
        quadrant(mine, kv_ref, slot, 0, 0, True, True, sums_ref)
        quadrant(mine, kv_ref, slot, 1, 1, True, False, sums_ref)
    else:
        full(mine, i * outer_count + o, False)

    @pl.when(odd == (0 if inner_back == 0 else 1))
    def _():
        full(other, (i + 1 - 2 * odd) * outer_count + o, False)


def own_kernel(off_ref, q_ref, do_ref, rows_ref, qp_ref, dop_ref, rowsp_ref, kv_ref, dq_ref, dqp_ref, sums_ref):
    sums_ref[...] = jnp.zeros_like(sums_ref)
    dqp_ref[...] = jnp.zeros_like(dqp_ref)
    mine = (q_ref, do_ref, rows_ref, dq_ref)
    other = (qp_ref, dop_ref, rowsp_ref, dqp_ref)
    visit(off_ref, mine, other, kv_ref, sums_ref, 0, 0, 0, True)


def store_part(part_ref, sums_ref, slot):
    part_ref[0] = (sums_ref[slot, 0] * SCALE).astype(BF16)
    part_ref[1] = sums_ref[slot, 1].astype(BF16)


def far_kernel(
    off_ref, q_ref, do_ref, rows_ref, qp_ref, dop_ref, rowsp_ref, kv_ref, dq_in, dqp_in, dq_ref, dqp_ref, part_ref, sums_ref
):
    sums_ref[...] = jnp.zeros_like(sums_ref)
    mine = (q_ref, do_ref, rows_ref, dq_ref)
    other = (qp_ref, dop_ref, rowsp_ref, dqp_ref)
    visit(off_ref, mine, other, kv_ref, sums_ref, 0, FAR, BACK, False)
    store_part(part_ref, sums_ref, 0)


def turned(dq_ref, half_at, pair):
    return (dq_ref[half_at, pair] * SCALE).T


def near_kernel(
    off_ref, q_ref, do_ref, rows_ref, qp_ref, dop_ref, rowsp_ref, kvz_ref, kvx_ref, dq_in, dqp_in,
    dq_ref, dqp_ref, partz_ref, partx_ref, pq_ref, sums_ref,
):
    sums_ref[...] = jnp.zeros_like(sums_ref)
    mine = (q_ref, do_ref, rows_ref, dq_ref)
    other = (qp_ref, dop_ref, rowsp_ref, dqp_ref)
    visit(off_ref, mine, other, kvz_ref, sums_ref, 0, 0, BACK, False)
    store_part(partz_ref, sums_ref, 0)
    visit(off_ref, mine, other, kvx_ref, sums_ref, 1, FAR, 0, False)
    store_part(partx_ref, sums_ref, 1)
    half = pq_ref.shape[0] // 2
    for side in range(2):
        for pair in range(dqp_ref.shape[1]):
            block = turned(dqp_ref, side, pair).astype(BF16)
            for j in range(2):
                h = 2 * pair + j
                pq_ref[side * half : (side + 1) * half, h * HEAD_WIDTH : (h + 1) * HEAD_WIDTH] = block[j * half : (j + 1) * half]


def query_kernel(dq_ref, recv_ref, keep_ref, send_ref):
    half = keep_ref.shape[0]
    me = lax.axis_index("head")
    for out_ref, side in ((send_ref, 1 - me), (keep_ref, me)):
        rows = pl.ds(pl.multiple_of(side * half, half), half)
        for pair in range(dq_ref.shape[1]):
            block = turned(dq_ref, side, pair)
            for j in range(2):
                h = 2 * pair + j
                cols = slice(h * HEAD_WIDTH, (h + 1) * HEAD_WIDTH)
                total = block[j * half : (j + 1) * half] + recv_ref[rows, cols].astype(F32)
                out_ref[:, cols] = total.astype(BF16)


def sum_kernel(own_ref, a_ref, b_ref, c_ref, keep_ref, send_ref):
    half = keep_ref.shape[1]
    me = lax.axis_index("head")
    for out_ref, side in ((send_ref, 1 - me), (keep_ref, me)):
        rows = pl.ds(pl.multiple_of(side * half, half), half)
        for at in range(2):
            own = own_ref[0, at, rows, :] * (SCALE if at == 0 else 1.0)
            total = own + a_ref[at, rows, :].astype(F32) + b_ref[at, rows, :].astype(F32) + c_ref[at, rows, :].astype(F32)
            out_ref[at] = total.astype(BF16)


def join_kernel(qk_ref, qr_ref, kk_ref, kr_ref, gq_ref, gk_ref, gv_ref):
    me = lax.axis_index("head")

    def put(out_ref, value, side, width):
        out_ref[0, :, pl.ds(pl.multiple_of(side * width, HEAD_WIDTH), width)] = value

    width = qk_ref.shape[1]
    put(gq_ref, qk_ref[...], me, width)
    put(gq_ref, qr_ref[...], 1 - me, width)
    width = kk_ref.shape[2]
    for at, out_ref in enumerate((gk_ref, gv_ref)):
        put(out_ref, kk_ref[at], me, width)
        put(out_ref, kr_ref[at], 1 - me, width)


def moved(value, inner_steps, outer_steps):
    inner_count, outer_count = lax.axis_size("inner"), lax.axis_size("outer")
    pairs = [
        (i * outer_count + o, (i + inner_steps) % inner_count * outer_count + (o + outer_steps) % outer_count)
        for i in range(inner_count)
        for o in range(outer_count)
    ]
    return lax.ppermute(value, ("inner", "outer"), pairs)


def swapped(value):
    return lax.ppermute(value, "inner", [(i, i ^ 1) for i in range(lax.axis_size("inner"))])


def crossed(value):
    return lax.ppermute(value, "head", [(0, 1), (1, 0)])


def struct(shape, dtype):
    return jax.ShapeDtypeStruct(shape, dtype)


def shards(queries, keys, values, grad_out, log_denominator, output_row_dot, offsets):
    _, tokens, query_cols = queries.shape
    kv_cols = keys.shape[2]
    heads = query_cols // HEAD_WIDTH
    half = tokens // 2
    q, do = queries[0], grad_out[0]
    norm, dots = log_denominator[0].T, output_row_dot[0].T

    kv, rows = call(
        prep_kernel,
        "prep",
        (struct((2, tokens, kv_cols), BF16), struct((2, 2, heads // 2, tokens), F32)),
        [VMEM] * 4,
        bytes_accessed=4 * tokens * kv_cols * 2,
    )(keys[0], values[0], norm, dots)

    kv_far = moved(kv, FAR, BACK)
    kv_back = moved(kv, 0, BACK)
    kv_side = moved(kv, FAR, 0)
    q_other, do_other, rows_other = swapped(q), swapped(do), swapped(rows)

    dq_shape = struct((2, heads // 2, HEAD_WIDTH, tokens), F32)
    part_shape = struct((2, tokens, kv_cols), BF16)
    sums_shape = (1, 2, tokens, kv_cols)
    base = (offsets, q, do, rows, q_other, do_other, rows_other)
    base_specs = [SMEM] + [VMEM] * 6
    flops = 2 * 2 * 5 * heads * tokens * tokens * HEAD_WIDTH

    dq, dq_other, own_sums = call(
        own_kernel, "own", (dq_shape, dq_shape, struct(sums_shape, F32)), base_specs + [VMEM], flops=flops, bytes_accessed=4 << 20
    )(*base, kv)
    dq, dq_other, part_far = call(
        far_kernel,
        "far",
        (dq_shape, dq_shape, part_shape),
        base_specs + [VMEM] * 3,
        flops=flops,
        bytes_accessed=4 << 20,
        aliases={8: 0, 9: 1},
        scratch=[pltpu.VMEM(sums_shape, F32)],
    )(*base, kv_far, dq, dq_other)
    back_far = moved(part_far, -FAR, -BACK)
    dq, dq_other, part_back, part_side, pq = call(
        near_kernel,
        "near",
        (dq_shape, dq_shape, part_shape, part_shape, struct((tokens, query_cols), BF16)),
        base_specs + [VMEM] * 4,
        flops=2 * flops,
        bytes_accessed=4 << 20,
        aliases={9: 0, 10: 1},
        scratch=[pltpu.VMEM((2,) + sums_shape[1:], F32)],
    )(*base, kv_back, kv_side, dq, dq_other)
    back_back = moved(part_back, 0, -BACK)
    back_side = moved(part_side, -FAR, 0)
    pq_other = swapped(pq)
    rows_shape = struct((half, query_cols), BF16)
    q_keep, q_send = call(query_kernel, "query", (rows_shape, rows_shape), [VMEM] * 2, bytes_accessed=2 << 20)(dq, pq_other)
    q_recv = crossed(q_send)
    kv_shape = struct((2, half, kv_cols), BF16)
    kv_keep, kv_send = call(sum_kernel, "sum", (kv_shape, kv_shape), [VMEM] * 4, bytes_accessed=1 << 20)(
        own_sums, back_far, back_back, back_side
    )
    kv_recv = crossed(kv_send)
    return call(
        join_kernel,
        "join",
        (struct((1, half, 2 * query_cols), BF16),) + (struct((1, half, 2 * kv_cols), BF16),) * 2,
        [VMEM] * 4,
        bytes_accessed=2 << 20,
    )(q_keep, q_recv, kv_keep, kv_recv)


def solution(mesh):
    split = P(("inner", "outer"), None, "head")
    joined = P(("inner", "outer"), "head", None)
    return jax.shard_map(
        shards,
        mesh=mesh,
        in_specs=(split,) * 6 + (P(),),
        out_specs=(joined,) * 3,
        check_vma=False,
    )
```

time: 102 us -> 45 us (0.44)
  waiting for transfers between devices: 32.4 us -> 12.2 us
  Pallas kernels: 0 us -> 14 us
  other arithmetic: 13 us -> 0 us
  matrix products: 12.2 us -> 0 us
  local copies, waits for them, and re-layouts: 15.3 us -> 4.6 us
  starting transfers between devices: 20.9 us -> 13.1 us
  blocking collectives: 6.49 us -> 0 us
    pallas_call x0 -> x7, Pallas kernels: none -> 14 us  [the longest x1 5.72 us: shards(): call(near_kernel, 'near', (dq_shape, dq_shape, part_shape, part_shape, st...]
    dot_general x30 -> x0, matrix products: 12.2 us -> none  [the longest x6 4.3 us: pair_terms(): jnp.einsum('gjtu,ugd->tgjd', scores_low, key_heads, preferred_element_typ...]
    add x9 -> x0, other arithmetic: 12.1 us -> none  [the longest x4 8.61 us: local_positions(): jnp.where(within < halfway, offset_row[0], offset_row[1]) + within % halfway]
    all_to_all x2 -> x0, waiting for transfers between devices: 10.2 us -> none  [the longest x1 8.56 us: shards(): lax.all_to_all(grad_query.astype(jnp.bfloat16), 'head', split_axis=0, con...]
    ppermute x11 -> x12, waiting for transfers between devices: 22.2 us -> 12.2 us  [the longest x6 5.89 us: moved(): return lax.ppermute(value, ('inner', 'outer'), pairs)]
    all_to_all x2 -> x0, starting transfers between devices: 6.79 us -> none  [the longest x1 3.49 us: shards(): lax.all_to_all(grad_query.astype(jnp.bfloat16), 'head', split_axis=0, con...]
    all_to_all x1 -> x0, blocking collectives: 6.49 us -> none  [shards(): lax.all_to_all(key_sums[0].astype(jnp.bfloat16), 'head', split_axis=0, co...]
    slice x13 -> x0, local copies, waits for them, and re-layouts: 5.4 us -> none  [the longest x7 3.85 us: local_positions(): offset_row[0]]
  transfers between devices with their start and end apart: 13 -> 12, of which waited for: 10 -> 5; matrix products, arithmetic and copies ran while one was open for 19% -> 0% of each run, Pallas kernels for 0% -> 16%
where the time goes in v1:
time: 45 us; the launch traced here: 44.7 us
  Pallas kernels  14 us (31%)
  starting transfers between devices  13.1 us (29%)
  waiting for transfers between devices  12.2 us (27%)
  local copies, waits for them, and re-layouts  4.6 us (10%)
  between operations  0.74 us (2%)
    ppermute x6, starting transfers between devices, moved(): return lax.ppermute(value, ('inner', 'outer'), pairs)  10.3 us
    ppermute x6, waiting for transfers between devices, moved(): return lax.ppermute(value, ('inner', 'outer'), pairs)  5.89 us
    pallas_call x1, Pallas kernels, shards(): call(near_kernel, 'near', (dq_shape, dq_shape, part_shape, part_shape, st...  5.72 us
    pallas_call x1, Pallas kernels, shards(): call(own_kernel, 'own', (dq_shape, dq_shape, struct(sums_shape, F32)), ba...  4.61 us
    unnamed x19, local copies, waits for them, and re-layouts  4.6 us
    ppermute x2, waiting for transfers between devices, crossed(): return lax.ppermute(value, 'head', [(0, 1), (1, 0)])  3.76 us
    ppermute x4, waiting for transfers between devices, swapped(): lax.ppermute(value, 'inner', [(i, i ^ 1) for i in range(lax.axis_size('in...  2.55 us
    pallas_call x1, Pallas kernels, shards(): call(far_kernel, 'far', (dq_shape, dq_shape, part_shape), base_specs + [V...  2.29 us
  transfers between devices with their start and end apart: 12, of which 5 were waited for; matrix products, arithmetic and copies ran while one was open for 0% of the time, Pallas kernels for 16%

profile of v1, /device:TPU:0, one launch (start us, length us, event | category | flops | bytes accessed | tf_op | source)
XLA Modules:
  0.0 44.7 jit_solution(10947361836866453595)
XLA Ops:
  0.6 0.0 copy-start.6
  0.6 0.6 %collective-permute-start = (bf16[128,2048]{1,0:T(8,128)(2,1)}, bf16[128,2048]{1,0:T(8,128)(2,1)S(1)}, u32[]{:S(2)}, u32[]{:S(2)}) collective-permute-start(bf16[128,2048]{1,0:T(8,128)(2,1)} %bitcast.10), channel_id=1, source_target_pairs={{0,4},{4,0},{8,12},{12,8},{1,5},{5,1},{9,13},{13,9},{2,6},{6,2},{1... | collective-permute-start | bytes 1572872 | tf_op jit(solution)/shard_map/ppermute | solution.py:238
  1.2 0.1 collective-permute-start.1
  1.3 0.0 copy-done.6
  1.3 0.0 copy-start.4
  1.3 0.8 %copy-done.4 = bf16[1,128,256]{2,1,0:T(8,128)(2,1)S(1)} copy-done((bf16[1,128,256]{2,1,0:T(8,128)(2,1)S(1)}, bf16[1,128,256]{2,1,0:T(8,128)(2,1)}, u32[]{:S(2)}) %copy-start.4) | copy-done | bytes 65560
  2.2 0.0 copy-start.5
  2.2 0.8 %copy-done.5 = bf16[1,128,256]{2,1,0:T(8,128)(2,1)S(1)} copy-done((bf16[1,128,256]{2,1,0:T(8,128)(2,1)S(1)}, bf16[1,128,256]{2,1,0:T(8,128)(2,1)}, u32[]{:S(2)}) %copy-start.5) | copy-done | bytes 65560
  3.0 0.0 copy-start.7
  3.0 0.7 %copy-done.7 = f32[1,128,16]{1,2,0:T(8,128)S(1)} copy-done((f32[1,128,16]{1,2,0:T(8,128)S(1)}, f32[1,128,16]{1,2,0:T(8,128)}, u32[]{:S(2)}) %copy-start.7) | copy-done | bytes 8216
  3.7 0.1 prep.1
  3.8 0.0 copy-start.8
  3.8 4.0 %collective-permute-start.5 = (bf16[2,128,256]{2,1,0:T(8,128)(2,1)S(1)}, bf16[2,128,256]{2,1,0:T(8,128)(2,1)S(1)}, u32[]{:S(2)}, u32[]{:S(2)}) collective-permute-start(bf16[2,128,256]{2,1,0:T(8,128)(2,1)S(1)} %get-tuple-element.20.kv_ref), channel_id=1, source_target_pairs={{0,9},{1,10},{2,11},{3,8},{4,13},{5,14},{6,15},{7,12},{8,1},{9,2},... | collective-permute-start | bytes 393224 | tf_op jit(solution)/shard_map/ppermute | solution.py:234
  7.8 0.0 collective-permute-start.2
  7.8 0.5 %collective-permute-start.4 = (bf16[2,128,256]{2,1,0:T(8,128)(2,1)S(1)}, bf16[2,128,256]{2,1,0:T(8,128)(2,1)S(1)}, u32[]{:S(2)}, u32[]{:S(2)}) collective-permute-start(bf16[2,128,256]{2,1,0:T(8,128)(2,1)S(1)} %get-tuple-element.20.kv_ref), channel_id=1, source_target_pairs={{0,8},{1,9},{2,10},{3,11},{4,12},{5,13},{6,14},{7,15},{8,0},{9,1},... | collective-permute-start | bytes 393224 | tf_op jit(solution)/shard_map/ppermute | solution.py:234
  8.3 0.6 %collective-permute-done.2.rowsp_ref = f32[2,2,8,128]{3,2,1,0:T(8,128)S(1)} collective-permute-done((f32[2,2,8,128]{3,2,1,0:T(8,128)S(1)}, f32[2,2,8,128]{3,2,1,0:T(8,128)S(1)}, u32[]{:S(2)}, u32[]{:S(2)}) %collective-permute-start.2) | collective-permute-done | bytes 16416 | tf_op jit(solution)/shard_map/ppermute | solution.py:238
  9.0 1.6 %collective-permute-start.3 = (bf16[2,128,256]{2,1,0:T(8,128)(2,1)S(1)}, bf16[2,128,256]{2,1,0:T(8,128)(2,1)S(1)}, u32[]{:S(2)}, u32[]{:S(2)}) collective-permute-start(bf16[2,128,256]{2,1,0:T(8,128)(2,1)S(1)} %get-tuple-element.20.kv_ref), channel_id=1, source_target_pairs={{0,1},{1,2},{2,3},{3,0},{4,5},{5,6},{6,7},{7,4},{8,9},{9,10},{10,1... | collective-permute-start | bytes 393224 | tf_op jit(solution)/shard_map/ppermute | solution.py:234
  10.5 0.0 copy-done.8
  10.5 0.1 copy.16.off_ref
  10.6 0.0 collective-permute-done.qp_ref
  10.6 0.0 collective-permute-done.1.dop_ref
  10.6 0.0 copy-start
  10.6 1.0 %copy-done = bf16[1,128,2048]{2,1,0:T(8,128)(2,1)S(1)} copy-done((bf16[1,128,2048]{2,1,0:T(8,128)(2,1)S(1)}, bf16[1,128,2048]{2,1,0:T(8,128)(2,1)}, u32[]{:S(2)}) %copy-start) | copy-done | bytes 524312
  11.7 0.0 copy-start.2
  11.7 1.0 %copy-done.2 = bf16[1,128,2048]{2,1,0:T(8,128)(2,1)S(1)} copy-done((bf16[1,128,2048]{2,1,0:T(8,128)(2,1)S(1)}, bf16[1,128,2048]{2,1,0:T(8,128)(2,1)}, u32[]{:S(2)}) %copy-start.2) | copy-done | bytes 524312
  12.7 4.6 %own.1 = (f32[2,8,128,128]{3,2,1,0:T(8,128)S(1)}, f32[2,8,128,128]{3,2,1,0:T(8,128)S(1)}, f32[1,2,128,256]{3,2,1,0:T(8,128)S(1)}) custom-call(s32[16,2]{1,0:T(8,128)S(1)} %copy.16.off_ref, bf16[128,2048]{1,0:T(8,128)(2,1)S(1)} %bitcast.11, bf16[128,2048]{1,0:T(8,128)(2,1)S(1)} %bitcast.15, f32[2,2,8,128]{3,2,1,0:T(8,128)S(1)} %get-tuple-element.19.rows_ref, ...), custom_call_target="tpu_custom_call" | custom-call | flops 671088640 | bytes 4194304 | tf_op jit(solution)/shard_map/own/pallas_call | solution.py:277
  17.3 0.0 collective-permute-done.5.kv_ref
  17.3 0.0 copy-done.1
  17.4 0.0 copy-done.3
  17.4 2.3 %far.1 = (f32[2,8,128,128]{3,2,1,0:T(8,128)S(1)}, f32[2,8,128,128]{3,2,1,0:T(8,128)S(1)}, bf16[2,128,256]{2,1,0:T(8,128)(2,1)S(1)}) custom-call(s32[16,2]{1,0:T(8,128)S(1)} %copy.16.off_ref, bf16[128,2048]{1,0:T(8,128)(2,1)S(1)} %bitcast.12, bf16[128,2048]{1,0:T(8,128)(2,1)S(1)} %bitcast.16, ...), custom_call_target="tpu_custom_call", output_to_operand_aliasing={{0}: (8, {}), {1}: (9, {})} | custom-call | flops 671088640 | bytes 4194304 | tf_op jit(solution)/shard_map/far/pallas_call | solution.py:280
  19.7 0.0 collective-permute-done.4.kvx_ref
  19.7 0.0 collective-permute-done.3.kvz_ref
  19.7 5.7 %near.1 = (f32[2,8,128,128]{3,2,1,0:T(8,128)S(1)}, f32[2,8,128,128]{3,2,1,0:T(8,128)S(1)}, bf16[2,128,256]{2,1,0:T(8,128)(2,1)S(1)}, bf16[2,128,256]{2,1,0:T(8,128)(2,1)S(1)}, bf16[128,2048]{1,0:T(8,128)(2,1)S(1)}) custom-call(s32[16,2]{1,0:T(8,128)S(1)} %copy.16.off_ref, ...), custom_call_target="tpu_custom_call", output_to_operand_aliasing={{0}: (9, {}), {1}: (10, {})} | custom-call | flops 1342177280 | bytes 4194304 | tf_op jit(solution)/shard_map/near/pallas_call | solution.py:291
  25.4 0.1 collective-permute-start.6
  25.5 1.9 %collective-permute-done.6.recv_ref = bf16[128,2048]{1,0:T(8,128)(2,1)S(1)} collective-permute-done((bf16[128,2048]{1,0:T(8,128)(2,1)S(1)}, bf16[128,2048]{1,0:T(8,128)(2,1)S(1)}, u32[]{:S(2)}, u32[]{:S(2)}) %collective-permute-start.6) | collective-permute-done | bytes 524320 | tf_op jit(solution)/shard_map/ppermute | solution.py:238
  27.4 0.3 query.1
  27.7 1.6 %collective-permute-start.7 = (bf16[64,2048]{1,0:T(8,128)(2,1)S(1)}, bf16[64,2048]{1,0:T(8,128)(2,1)S(1)}, u32[]{:S(2)}, u32[]{:S(2)}) collective-permute-start(bf16[64,2048]{1,0:T(8,128)(2,1)S(1)} %get-tuple-element.28), channel_id=1, source_target_pairs={{0,16},{16,0},{1,17},{17,1},{2,18},{18,2},{3,19},{19,3},{4,20},{20... | collective-permute-start | bytes 786440 | tf_op jit(solution)/shard_map/ppermute | solution.py:242
  29.3 2.2 %collective-permute-start.9 = (bf16[2,128,256]{2,1,0:T(8,128)(2,1)S(1)}, bf16[2,128,256]{2,1,0:T(8,128)(2,1)S(1)}, u32[]{:S(2)}, u32[]{:S(2)}) collective-permute-start(bf16[2,128,256]{2,1,0:T(8,128)(2,1)S(1)} %get-tuple-element.31), channel_id=1, source_target_pairs={{0,3},{1,0},{2,1},{3,2},{4,7},{5,4},{6,5},{7,6},{8,11},{9,8},{10,9... | collective-permute-start | bytes 393224 | tf_op jit(solution)/shard_map/ppermute | solution.py:234
  31.6 0.8 %collective-permute-start.10 = (bf16[2,128,256]{2,1,0:T(8,128)(2,1)S(1)}, bf16[2,128,256]{2,1,0:T(8,128)(2,1)S(1)}, u32[]{:S(2)}, u32[]{:S(2)}) collective-permute-start(bf16[2,128,256]{2,1,0:T(8,128)(2,1)S(1)} %get-tuple-element.32), channel_id=1, source_target_pairs={{0,8},{1,9},{2,10},{3,11},{4,12},{5,13},{6,14},{7,15},{8,0},{9,1},... | collective-permute-start | bytes 393224 | tf_op jit(solution)/shard_map/ppermute | solution.py:234
  32.4 1.1 %collective-permute-start.8 = (bf16[2,128,256]{2,1,0:T(8,128)(2,1)S(1)}, bf16[2,128,256]{2,1,0:T(8,128)(2,1)S(1)}, u32[]{:S(2)}, u32[]{:S(2)}) collective-permute-start(bf16[2,128,256]{2,1,0:T(8,128)(2,1)S(1)} %get-tuple-element.30), channel_id=1, source_target_pairs={{0,11},{1,8},{2,9},{3,10},{4,15},{5,12},{6,13},{7,14},{8,3},{9,0},... | collective-permute-start | bytes 393224 | tf_op jit(solution)/shard_map/ppermute | solution.py:234
  33.5 2.0 %collective-permute-done.9.b_ref = bf16[2,128,256]{2,1,0:T(8,128)(2,1)S(1)} collective-permute-done((bf16[2,128,256]{2,1,0:T(8,128)(2,1)S(1)}, bf16[2,128,256]{2,1,0:T(8,128)(2,1)S(1)}, u32[]{:S(2)}, u32[]{:S(2)}) %collective-permute-start.9) | collective-permute-done | bytes 131104 | tf_op jit(solution)/shard_map/ppermute | solution.py:234
  35.5 3.9 %collective-permute-done.10.c_ref = bf16[2,128,256]{2,1,0:T(8,128)(2,1)S(1)} collective-permute-done((bf16[2,128,256]{2,1,0:T(8,128)(2,1)S(1)}, bf16[2,128,256]{2,1,0:T(8,128)(2,1)S(1)}, u32[]{:S(2)}, u32[]{:S(2)}) %collective-permute-start.10) | collective-permute-done | bytes 131104 | tf_op jit(solution)/shard_map/ppermute | solution.py:234
  39.4 0.0 collective-permute-done.8.a_ref
  39.4 0.1 sum.1
  39.4 0.6 %collective-permute-start.11 = (bf16[2,64,256]{2,1,0:T(8,128)(2,1)S(1)}, bf16[2,64,256]{2,1,0:T(8,128)(2,1)S(1)}, u32[]{:S(2)}, u32[]{:S(2)}) collective-permute-start(bf16[2,64,256]{2,1,0:T(8,128)(2,1)S(1)} %get-tuple-element.34), channel_id=1, source_target_pairs={{0,16},{16,0},{1,17},{17,1},{2,18},{18,2},{3,19},{19,3},{4,20},{20... | collective-permute-start | bytes 196616 | tf_op jit(solution)/shard_map/ppermute | solution.py:242
  40.0 3.8 %collective-permute-done.11.kr_ref = bf16[2,64,256]{2,1,0:T(8,128)(2,1)S(1)} collective-permute-done((bf16[2,64,256]{2,1,0:T(8,128)(2,1)S(1)}, bf16[2,64,256]{2,1,0:T(8,128)(2,1)S(1)}, u32[]{:S(2)}, u32[]{:S(2)}) %collective-permute-start.11) | collective-permute-done | bytes 65568 | tf_op jit(solution)/shard_map/ppermute | solution.py:242
  43.8 0.0 collective-permute-done.7.qr_ref
  43.8 0.9 %join.1 = (bf16[1,64,4096]{2,1,0:T(8,128)(2,1)}, bf16[1,64,512]{2,1,0:T(8,128)(2,1)}, bf16[1,64,512]{2,1,0:T(8,128)(2,1)}) custom-call(bf16[64,2048]{1,0:T(8,128)(2,1)S(1)} %get-tuple-element.27.qk_ref, bf16[64,2048]{1,0:T(8,128)(2,1)S(1)} %collective-permute-done.7.qr_ref, bf16[2,64,256]{2,1,0:T(8,128)(2,1)S(1)} %get-tuple-element.33.kk_ref, ...), custom_call_target="tpu_custom_call" | custom-call | bytes 2097152 | tf_op jit(solution)/shard_map/join/pallas_call | solution.py:312
  (2 shorter events, 0.0 us)
Async XLA Ops:
  0.6 0.7 %copy-start.6 = (f32[1,128,16]{1,2,0:T(8,128)S(1)}, f32[1,128,16]{1,2,0:T(8,128)}, u32[]{:S(2)}) copy-start(f32[1,128,16]{1,2,0:T(8,128)} %param.11) | copy-start | bytes 24580
  0.6 10.0 %collective-permute-start = (bf16[128,2048]{1,0:T(8,128)(2,1)}, bf16[128,2048]{1,0:T(8,128)(2,1)S(1)}, u32[]{:S(2)}, u32[]{:S(2)}) collective-permute-start(bf16[128,2048]{1,0:T(8,128)(2,1)} %bitcast.10), channel_id=1, source_target_pairs={{0,4},{4,0},{8,12},{12,8},{1,5},{5,1},{9,13},{13,9},{2,6},{6,2},{1... | collective-permute-start | bytes 1572872 | tf_op jit(solution)/shard_map/ppermute | solution.py:238
  1.2 9.4 %collective-permute-start.1 = (bf16[128,2048]{1,0:T(8,128)(2,1)}, bf16[128,2048]{1,0:T(8,128)(2,1)S(1)}, u32[]{:S(2)}, u32[]{:S(2)}) collective-permute-start(bf16[128,2048]{1,0:T(8,128)(2,1)} %bitcast.14), channel_id=1, source_target_pairs={{0,4},{4,0},{8,12},{12,8},{1,5},{5,1},{9,13},{13,9},{2,6},{6,2},{1... | collective-permute-start | bytes 1572872 | tf_op jit(solution)/shard_map/ppermute | solution.py:238
  1.3 0.8 %copy-start.4 = (bf16[1,128,256]{2,1,0:T(8,128)(2,1)S(1)}, bf16[1,128,256]{2,1,0:T(8,128)(2,1)}, u32[]{:S(2)}) copy-start(bf16[1,128,256]{2,1,0:T(8,128)(2,1)} %param.8) | copy-start | bytes 196612
  2.2 0.8 %copy-start.5 = (bf16[1,128,256]{2,1,0:T(8,128)(2,1)S(1)}, bf16[1,128,256]{2,1,0:T(8,128)(2,1)}, u32[]{:S(2)}) copy-start(bf16[1,128,256]{2,1,0:T(8,128)(2,1)} %param.9) | copy-start | bytes 196612
  3.0 0.7 %copy-start.7 = (f32[1,128,16]{1,2,0:T(8,128)S(1)}, f32[1,128,16]{1,2,0:T(8,128)}, u32[]{:S(2)}) copy-start(f32[1,128,16]{1,2,0:T(8,128)} %param.12) | copy-start | bytes 24580
  3.8 6.8 %copy-start.8 = (s32[16,2]{0,1:T(2,128)S(1)}, s32[16,2]{0,1:T(2,128)}, u32[]{:S(2)}) copy-start(s32[16,2]{0,1:T(2,128)} %param.13) | copy-start | bytes 388
  3.8 13.6 %collective-permute-start.5 = (bf16[2,128,256]{2,1,0:T(8,128)(2,1)S(1)}, bf16[2,128,256]{2,1,0:T(8,128)(2,1)S(1)}, u32[]{:S(2)}, u32[]{:S(2)}) collective-permute-start(bf16[2,128,256]{2,1,0:T(8,128)(2,1)S(1)} %get-tuple-element.20.kv_ref), channel_id=1, source_target_pairs={{0,9},{1,10},{2,11},{3,8},{4,13},{5,14},{6,15},{7,12},{8,1},{9,2},... | collective-permute-start | bytes 393224 | tf_op jit(solution)/shard_map/ppermute | solution.py:234
  7.8 1.2 %collective-permute-start.2 = (f32[2,2,8,128]{3,2,1,0:T(8,128)S(1)}, f32[2,2,8,128]{3,2,1,0:T(8,128)S(1)}, u32[]{:S(2)}, u32[]{:S(2)}) collective-permute-start(f32[2,2,8,128]{3,2,1,0:T(8,128)S(1)} %get-tuple-element.19.rows_ref), channel_id=1, source_target_pairs={{0,4},{4,0},{8,12},{12,8},{1,5},{5,1},{9,13},{13,9},{2,6},{6,2},{1... | collective-permute-start | bytes 49160 | tf_op jit(solution)/shard_map/ppermute | solution.py:238
  7.8 11.9 %collective-permute-start.4 = (bf16[2,128,256]{2,1,0:T(8,128)(2,1)S(1)}, bf16[2,128,256]{2,1,0:T(8,128)(2,1)S(1)}, u32[]{:S(2)}, u32[]{:S(2)}) collective-permute-start(bf16[2,128,256]{2,1,0:T(8,128)(2,1)S(1)} %get-tuple-element.20.kv_ref), channel_id=1, source_target_pairs={{0,8},{1,9},{2,10},{3,11},{4,12},{5,13},{6,14},{7,15},{8,0},{9,1},... | collective-permute-start | bytes 393224 | tf_op jit(solution)/shard_map/ppermute | solution.py:234
  9.0 10.7 %collective-permute-start.3 = (bf16[2,128,256]{2,1,0:T(8,128)(2,1)S(1)}, bf16[2,128,256]{2,1,0:T(8,128)(2,1)S(1)}, u32[]{:S(2)}, u32[]{:S(2)}) collective-permute-start(bf16[2,128,256]{2,1,0:T(8,128)(2,1)S(1)} %get-tuple-element.20.kv_ref), channel_id=1, source_target_pairs={{0,1},{1,2},{2,3},{3,0},{4,5},{5,6},{6,7},{7,4},{8,9},{9,10},{10,1... | collective-permute-start | bytes 393224 | tf_op jit(solution)/shard_map/ppermute | solution.py:234
  10.6 1.0 %copy-start = (bf16[1,128,2048]{2,1,0:T(8,128)(2,1)S(1)}, bf16[1,128,2048]{2,1,0:T(8,128)(2,1)}, u32[]{:S(2)}) copy-start(bf16[1,128,2048]{2,1,0:T(8,128)(2,1)} %param.7) | copy-start | bytes 1572868
  11.7 1.0 %copy-start.2 = (bf16[1,128,2048]{2,1,0:T(8,128)(2,1)S(1)}, bf16[1,128,2048]{2,1,0:T(8,128)(2,1)}, u32[]{:S(2)}) copy-start(bf16[1,128,2048]{2,1,0:T(8,128)(2,1)} %param.10) | copy-start | bytes 1572868
  12.7 4.6 %copy-start.1 = (bf16[1,128,2048]{2,1,0:T(8,128)(2,1)S(1)}, bf16[1,128,2048]{2,1,0:T(8,128)(2,1)}, u32[]{:S(2)}) copy-start(bf16[1,128,2048]{2,1,0:T(8,128)(2,1)} %param.7) | copy-start | bytes 1572868
  12.7 4.6 %copy-start.3 = (bf16[1,128,2048]{2,1,0:T(8,128)(2,1)S(1)}, bf16[1,128,2048]{2,1,0:T(8,128)(2,1)}, u32[]{:S(2)}) copy-start(bf16[1,128,2048]{2,1,0:T(8,128)(2,1)} %param.10) | copy-start | bytes 1572868
  25.4 2.0 %collective-permute-start.6 = (bf16[128,2048]{1,0:T(8,128)(2,1)S(1)}, bf16[128,2048]{1,0:T(8,128)(2,1)S(1)}, u32[]{:S(2)}, u32[]{:S(2)}) collective-permute-start(bf16[128,2048]{1,0:T(8,128)(2,1)S(1)} %get-tuple-element.26), channel_id=1, source_target_pairs={{0,4},{4,0},{8,12},{12,8},{1,5},{5,1},{9,13},{13,9},{2,6},{6,2},{1... | collective-permute-start | bytes 1572872 | tf_op jit(solution)/shard_map/ppermute | solution.py:238
  27.7 16.0 %collective-permute-start.7 = (bf16[64,2048]{1,0:T(8,128)(2,1)S(1)}, bf16[64,2048]{1,0:T(8,128)(2,1)S(1)}, u32[]{:S(2)}, u32[]{:S(2)}) collective-permute-start(bf16[64,2048]{1,0:T(8,128)(2,1)S(1)} %get-tuple-element.28), channel_id=1, source_target_pairs={{0,16},{16,0},{1,17},{17,1},{2,18},{18,2},{3,19},{19,3},{4,20},{20... | collective-permute-start | bytes 786440 | tf_op jit(solution)/shard_map/ppermute | solution.py:242
  29.3 6.1 %collective-permute-start.9 = (bf16[2,128,256]{2,1,0:T(8,128)(2,1)S(1)}, bf16[2,128,256]{2,1,0:T(8,128)(2,1)S(1)}, u32[]{:S(2)}, u32[]{:S(2)}) collective-permute-start(bf16[2,128,256]{2,1,0:T(8,128)(2,1)S(1)} %get-tuple-element.31), channel_id=1, source_target_pairs={{0,3},{1,0},{2,1},{3,2},{4,7},{5,4},{6,5},{7,6},{8,11},{9,8},{10,9... | collective-permute-start | bytes 393224 | tf_op jit(solution)/shard_map/ppermute | solution.py:234
  31.6 7.8 %collective-permute-start.10 = (bf16[2,128,256]{2,1,0:T(8,128)(2,1)S(1)}, bf16[2,128,256]{2,1,0:T(8,128)(2,1)S(1)}, u32[]{:S(2)}, u32[]{:S(2)}) collective-permute-start(bf16[2,128,256]{2,1,0:T(8,128)(2,1)S(1)} %get-tuple-element.32), channel_id=1, source_target_pairs={{0,8},{1,9},{2,10},{3,11},{4,12},{5,13},{6,14},{7,15},{8,0},{9,1},... | collective-permute-start | bytes 393224 | tf_op jit(solution)/shard_map/ppermute | solution.py:234
  32.4 6.9 %collective-permute-start.8 = (bf16[2,128,256]{2,1,0:T(8,128)(2,1)S(1)}, bf16[2,128,256]{2,1,0:T(8,128)(2,1)S(1)}, u32[]{:S(2)}, u32[]{:S(2)}) collective-permute-start(bf16[2,128,256]{2,1,0:T(8,128)(2,1)S(1)} %get-tuple-element.30), channel_id=1, source_target_pairs={{0,11},{1,8},{2,9},{3,10},{4,15},{5,12},{6,13},{7,14},{8,3},{9,0},... | collective-permute-start | bytes 393224 | tf_op jit(solution)/shard_map/ppermute | solution.py:234
  39.4 4.3 %collective-permute-start.11 = (bf16[2,64,256]{2,1,0:T(8,128)(2,1)S(1)}, bf16[2,64,256]{2,1,0:T(8,128)(2,1)S(1)}, u32[]{:S(2)}, u32[]{:S(2)}) collective-permute-start(bf16[2,64,256]{2,1,0:T(8,128)(2,1)S(1)} %get-tuple-element.34), channel_id=1, source_target_pairs={{0,16},{16,0},{1,17},{17,1},{2,18},{18,2},{3,19},{19,3},{4,20},{20... | collective-permute-start | bytes 196616 | tf_op jit(solution)/shard_map/ppermute | solution.py:242

commit v2 on v1

v2 whole, which is shorter than its diff:
```python
import math

import jax
import jax.numpy as jnp
from jax import lax
from jax.experimental import pallas as pl
from jax.experimental.pallas import tpu as pltpu
from jax.sharding import PartitionSpec as P


HEAD_WIDTH = 128
FAR = 2
BACK = 1

SCALE = 1.0 / math.sqrt(HEAD_WIDTH)
VMEM = pl.BlockSpec(memory_space=pltpu.VMEM)
HBM = pl.BlockSpec(memory_space=pltpu.HBM)
SMEM = pl.BlockSpec(memory_space=pltpu.SMEM)
F32 = jnp.float32
BF16 = jnp.bfloat16
VMEM_LIMIT = 24 * 1024 * 1024


def dot_nt(a, b):
    return lax.dot_general(a, b, (((1,), (1,)), ((), ())), preferred_element_type=F32)


def dot_nn(a, b):
    return lax.dot_general(a, b, (((1,), (0,)), ((), ())), preferred_element_type=F32)


def call(kernel, out_shape, in_specs, *, flops=0, bytes_accessed=0, aliases=None, scratch=(), out_space=None):
    return pl.pallas_call(
        kernel,
        out_shape=out_shape,
        in_specs=in_specs,
        out_specs=jax.tree.map(lambda _: out_space or VMEM, out_shape),
        scratch_shapes=scratch,
        input_output_aliases=aliases or {},
        cost_estimate=pl.CostEstimate(flops=flops, bytes_accessed=bytes_accessed, transcendentals=0),
        compiler_params=pltpu.CompilerParams(vmem_limit_bytes=VMEM_LIMIT),
    )


LOG2E = math.log2(math.e)


def prep_kernel(k_hbm, v_hbm, norm_hbm, dot_hbm, kv_ref, rows_ref, raw_ref, sems):
    copies = [
        pltpu.make_async_copy(source, target, sems.at[at])
        for at, (source, target) in enumerate(
            ((k_hbm, kv_ref.at[0]), (v_hbm, kv_ref.at[1]), (norm_hbm, raw_ref.at[0]), (dot_hbm, raw_ref.at[1]))
        )
    ]
    for copy in copies:
        copy.start()
    for copy in copies:
        copy.wait()
    heads, tokens = raw_ref.shape[1:]
    half = tokens // 2
    lanes = lax.broadcasted_iota(jnp.int32, (heads // 2, tokens), 1)
    for at, factor in enumerate((LOG2E, 1.0)):
        even = raw_ref[at, pl.ds(0, heads // 2, stride=2), :] * factor
        odd = raw_ref[at, pl.ds(1, heads // 2, stride=2), :] * factor
        rows_ref[at, 0] = jnp.where(lanes < half, even, pltpu.roll(odd, half, 1))
        rows_ref[at, 1] = jnp.where(lanes < half, pltpu.roll(even, half, 1), odd)


CHUNK = 4


def half_rows(which, half):
    if isinstance(which, int):
        return pl.ds(which * half, half)
    return pl.ds(pl.multiple_of(which * half, half), half)


def attend(query, g, query_half, blocks, sums_ref, diagonal=False):
    q_ref, do_ref, rows_ref, ds_ref = query
    half = q_ref.shape[0] // 2
    heads_kv = sums_ref.shape[-1] // HEAD_WIDTH
    per_group = q_ref.shape[1] // HEAD_WIDTH // heads_kv
    kv_cols = slice(g * HEAD_WIDTH, (g + 1) * HEAD_WIDTH)
    query_rows = half_rows(query_half, half)
    k = jnp.concatenate([kv_ref[0, half_rows(at, half), kv_cols] for kv_ref, at, _, _ in blocks], 0)
    v = jnp.concatenate([kv_ref[1, half_rows(at, half), kv_cols] for kv_ref, at, _, _ in blocks], 0)
    if diagonal:
        u = lax.broadcasted_iota(jnp.int32, (half, CHUNK * half), 0)
        t = lax.broadcasted_iota(jnp.int32, (half, CHUNK * half), 1) % half
        visible = u <= t
    queries, grads, probs, scores = [], [], [], []
    for c in range(per_group // CHUNK):
        heads = [g * per_group + c * CHUNK + j for j in range(CHUNK)]
        qc = jnp.concatenate([q_ref[query_rows, h * HEAD_WIDTH : (h + 1) * HEAD_WIDTH] for h in heads], 0)
        doc = jnp.concatenate([do_ref[query_rows, h * HEAD_WIDTH : (h + 1) * HEAD_WIDTH] for h in heads], 0)
        pairs = [heads[0] // 2 + i for i in range(CHUNK // 2)]
        norm = jnp.concatenate([rows_ref[0, query_half, pl.ds(p, 1), :] for p in pairs], 1)
        dots = jnp.concatenate([rows_ref[1, query_half, pl.ds(p, 1), :] for p in pairs], 1)
        prob = jnp.exp2(dot_nt(k, qc) * (SCALE * LOG2E) - norm)
        if diagonal:
            prob = jnp.where(visible, prob, 0.0)
        queries.append(qc)
        grads.append(doc)
        probs.append(prob.astype(BF16))
        scores.append((prob * (dot_nt(v, doc) - dots)).astype(BF16))
    score = jnp.concatenate(scores, 1)
    dv = dot_nn(jnp.concatenate(probs, 1), jnp.concatenate(grads, 0))
    dk = dot_nn(score, jnp.concatenate(queries, 0))
    width = score.shape[1]
    for at, (_, key_half, slot, score_slot) in enumerate(blocks):
        mine = slice(at * half, (at + 1) * half)
        sums_ref[slot, 0, half_rows(key_half, half), kv_cols] += dk[mine]
        sums_ref[slot, 1, half_rows(key_half, half), kv_cols] += dv[mine]
        ds_ref[score_slot, :, g * width : (g + 1) * width] = score[mine]


def wrapped(index, steps, count):
    moved = index - steps
    return jnp.where(moved < 0, moved + count, moved)


def block_of(inner_back, outer_back):
    inner_count, outer_count = lax.axis_size("inner"), lax.axis_size("outer")
    inner = wrapped(lax.axis_index("inner"), inner_back, inner_count)
    return inner * outer_count + wrapped(lax.axis_index("outer"), outer_back, outer_count)


def partner_block():
    i = lax.axis_index("inner")
    return (i + 1 - 2 * (i & 1)) * lax.axis_size("outer") + lax.axis_index("outer")


def is_odd():
    return lax.axis_index("inner") & 1


def visit(query, kv_ref, side, slot, sums_ref, sums_slot):
    ds_ref = query[3]
    slots = ds_ref.shape[0] // 3
    ds_ref[(2 - side) * slots + slot] = jnp.zeros(ds_ref.shape[1:], ds_ref.dtype)
    for g in range(sums_ref.shape[-1] // HEAD_WIDTH):
        attend(query, g, 1, [(kv_ref, 0, sums_slot, slot)], sums_ref)
        attend(query, g, side, [(kv_ref, side, sums_slot, (1 + side) * slots + slot)], sums_ref)


SIDE, BACK_SELF, FAR_SELF, OTHER_FIRST, OTHER_SECOND = range(5)


def write_flags(flags_ref, off_ref):
    odd = is_odd()
    own, other = block_of(0, 0), partner_block()
    side, back, far = block_of(FAR, 0), block_of(0, BACK), block_of(FAR, BACK)
    pairs = (
        (side, own),
        (back, own),
        (far, own),
        (jnp.where(odd == 1, side, back), other),
        (jnp.where(odd == 1, far, own), other),
    )
    for row, (keys, queries) in enumerate(pairs):
        flag = jnp.where(off_ref[0, keys] < off_ref[0, queries], 0, 1)
        flags_ref[pl.ds(row, 1), :] = jnp.full((1, flags_ref.shape[1]), flag, jnp.int32)


def flag_of(flags_ref, row):
    return jnp.max(flags_ref[pl.ds(row, 1), :])


def own_kernel(off_hbm, q_hbm, do_hbm, rows_ref, kv_ref, q_ref, do_ref, flags_ref, ds_ref, sums_ref, off_ref, off_sem, sems):
    groups = kv_ref.shape[-1] // HEAD_WIDTH
    width = q_ref.shape[1] // groups
    copies = [
        [
            pltpu.make_async_copy(
                source.at[:, g * width : (g + 1) * width], target.at[:, g * width : (g + 1) * width], sems.at[at, g]
            )
            for at, (source, target) in enumerate(((q_hbm, q_ref), (do_hbm, do_ref)))
        ]
        for g in range(groups)
    ]
    for pair in copies:
        for copy in pair:
            copy.start()
    offsets = pltpu.make_async_copy(off_hbm, off_ref, off_sem)
    offsets.start()
    sums_ref[...] = jnp.zeros_like(sums_ref)
    mine = (q_ref, do_ref, rows_ref, ds_ref)
    slots = ds_ref.shape[0] // 3
    for g in range(groups):
        for copy in copies[g]:
            copy.wait()
        attend(mine, g, 1, [(kv_ref, 0, 0, 0)], sums_ref)
        attend(mine, g, 0, [(kv_ref, 0, 0, slots)], sums_ref, diagonal=True)
        attend(mine, g, 1, [(kv_ref, 1, 0, 2 * slots)], sums_ref, diagonal=True)
    offsets.wait()
    write_flags(flags_ref, off_ref)


def store_part(part_ref, sums_ref, slot):
    part_ref[0] = (sums_ref[slot, 0] * SCALE).astype(BF16)
    part_ref[1] = sums_ref[slot, 1].astype(BF16)


def side_kernel(flags_ref, q_ref, do_ref, rows_ref, kv_ref, ds_in, ds_ref, sums_ref):
    sums_ref[...] = jnp.zeros_like(sums_ref)
    visit((q_ref, do_ref, rows_ref, ds_ref), kv_ref, flag_of(flags_ref, SIDE), 1, sums_ref, 0)


def back_kernel(
    flags_ref, q_ref, do_ref, rows_ref, qp_ref, dop_ref, rowsp_ref, side_ref, kv_ref, side_sums, ds_in,
    ds_ref, dsp_ref, parts_ref, partb_ref, keys_ref, sums_ref,
):
    sums_ref[0] = jnp.zeros(sums_ref.shape[1:], F32)
    sums_ref[1] = side_sums[0]
    odd = is_odd()
    keys_ref[...] = jnp.where(odd == 1, side_ref[...], kv_ref[...])
    visit((q_ref, do_ref, rows_ref, ds_ref), kv_ref, flag_of(flags_ref, BACK_SELF), 2, sums_ref, 0)
    visit((qp_ref, dop_ref, rowsp_ref, dsp_ref), keys_ref, flag_of(flags_ref, OTHER_FIRST), 0, sums_ref, odd)
    store_part(partb_ref, sums_ref, 0)
    store_part(parts_ref, sums_ref, 1)


def query_grads(ds_ref, early_keys, late_keys, put):
    slots = ds_ref.shape[0] // 3
    half = ds_ref.shape[1]
    groups = early_keys.shape[-1] // HEAD_WIDTH
    width = ds_ref.shape[2] // groups
    for g in range(groups):
        cols = slice(g * HEAD_WIDTH, (g + 1) * HEAD_WIDTH)
        early, late = early_keys[:, cols], late_keys[:, cols]
        both = jnp.concatenate([early, late], 0).T

        def scores(region):
            return ds_ref[region * slots : (region + 1) * slots, :, g * width : (g + 1) * width].reshape(slots * half, width)

        for side in range(2):
            if side == 0:
                total = dot_nn(both[:, : slots * half], scores(1))
            else:
                total = dot_nn(both, jnp.concatenate([scores(0), scores(2)], 0))
            total = total * SCALE
            for pair in range(width // (2 * half)):
                block = total[:, pair * 2 * half : (pair + 1) * 2 * half].T
                head = (g * width // half) + 2 * pair
                for j in range(2):
                    put(side, head + j, block[j * half : (j + 1) * half])


def stacked(kvs, half):
    return [jnp.concatenate([kv[0, side * half : (side + 1) * half, :] for kv in kvs], 0) for side in range(2)]


def far_kernel(
    flags_ref, q_ref, do_ref, rows_ref, qp_ref, dop_ref, rowsp_ref, own_ref, kv_ref, first_ref, own_sums, ds_in, dsp_in,
    ds_ref, dsp_ref, owns_ref, part_ref, pq_ref, keys_ref, sums_ref,
):
    sums_ref[0] = jnp.zeros(sums_ref.shape[1:], F32)
    sums_ref[1] = own_sums[0]
    odd = is_odd()
    half = ds_ref.shape[1]
    keys_ref[...] = jnp.where(odd == 1, kv_ref[...], own_ref[...])
    visit((qp_ref, dop_ref, rowsp_ref, dsp_ref), keys_ref, flag_of(flags_ref, OTHER_SECOND), 1, sums_ref, 1 - odd)
    visit((q_ref, do_ref, rows_ref, ds_ref), kv_ref, flag_of(flags_ref, FAR_SELF), 3, sums_ref, 0)
    store_part(part_ref, sums_ref, 0)
    owns_ref[...] = sums_ref[1]
    early, late = stacked([first_ref, keys_ref], half)

    def put(side, head, block):
        pq_ref[side * half : (side + 1) * half, head * HEAD_WIDTH : (head + 1) * HEAD_WIDTH] = block.astype(BF16)

    query_grads(dsp_ref, early, late, put)


def mine_kernel(ds_ref, own_ref, side_ref, back_ref, far_ref, mine_ref):
    half = ds_ref.shape[1]
    early, late = stacked([own_ref, side_ref, back_ref, far_ref], half)

    def put(side, head, block):
        mine_ref[side, :, head * HEAD_WIDTH : (head + 1) * HEAD_WIDTH] = block

    query_grads(ds_ref, early, late, put)


def query_kernel(mine_ref, recv_ref, keep_ref, send_ref):
    half = keep_ref.shape[0]
    me = lax.axis_index("head")
    for out_ref, side in ((send_ref, 1 - me), (keep_ref, me)):
        out_ref[...] = (mine_ref[side] + recv_ref[half_rows(side, half), :].astype(F32)).astype(BF16)


def sum_kernel(own_ref, a_ref, b_ref, c_ref, keep_ref, send_ref):
    half = keep_ref.shape[1]
    me = lax.axis_index("head")
    for out_ref, side in ((send_ref, 1 - me), (keep_ref, me)):
        rows = pl.ds(pl.multiple_of(side * half, half), half)
        for at in range(2):
            own = own_ref[at, rows, :] * (SCALE if at == 0 else 1.0)
            total = own + a_ref[at, rows, :].astype(F32) + b_ref[at, rows, :].astype(F32) + c_ref[at, rows, :].astype(F32)
            out_ref[at] = total.astype(BF16)


def join_kernel(sems, *pairs):
    me = lax.axis_index("head")
    copies = []
    for at, (kept, received, joined) in enumerate(pairs):
        width = kept.shape[-1]
        for j, (source, side) in enumerate(((kept, me), (received, 1 - me))):
            cols = pl.ds(pl.multiple_of(side * width, HEAD_WIDTH), width)
            copies.append(pltpu.make_async_copy(source, joined.at[0, :, cols], sems.at[at, j]))
    for copy in copies:
        copy.start()
    for copy in copies:
        copy.wait()


def join_query_kernel(kept, received, joined, sems):
    join_kernel(sems, (kept, received, joined))


def join_keys_kernel(kept, received, joined_k, joined_v, sems):
    join_kernel(sems, (kept.at[0], received.at[0], joined_k), (kept.at[1], received.at[1], joined_v))


def moved(value, inner_steps, outer_steps):
    inner_count, outer_count = lax.axis_size("inner"), lax.axis_size("outer")
    pairs = [
        (i * outer_count + o, (i + inner_steps) % inner_count * outer_count + (o + outer_steps) % outer_count)
        for i in range(inner_count)
        for o in range(outer_count)
    ]
    return lax.ppermute(value, ("inner", "outer"), pairs)


def swapped(value):
    return lax.ppermute(value, "inner", [(i, i ^ 1) for i in range(lax.axis_size("inner"))])


def crossed(value):
    return lax.ppermute(value, "head", [(0, 1), (1, 0)])


def in_hbm(value):
    return pltpu.with_memory_space_constraint(value, pltpu.HBM)


def struct(shape, dtype):
    return jax.ShapeDtypeStruct(shape, dtype)


def program(queries, keys, values, grad_out, log_denominator, output_row_dot, offsets):
    _, tokens, query_cols = queries.shape
    kv_cols = keys.shape[2]
    heads = query_cols // HEAD_WIDTH
    half = tokens // 2
    q, do = queries[0], grad_out[0]
    norm, dots = log_denominator[0].T, output_row_dot[0].T

    kv, rows = call(
        prep_kernel,
        (struct((2, tokens, kv_cols), BF16), struct((2, 2, heads // 2, tokens), F32)),
        [HBM] * 4,
        bytes_accessed=4 * tokens * kv_cols * 2,
        scratch=[pltpu.VMEM((2, heads, tokens), F32), pltpu.SemaphoreType.DMA((4,))],
    )(*(in_hbm(x) for x in (keys[0], values[0], norm, dots)))

    kv_back = moved(kv, 0, BACK)
    kv_side = moved(kv, FAR, 0)
    kv_far = moved(kv_back, FAR, 0)
    q_other, do_other, rows_other = swapped(q), swapped(do), swapped(rows)

    block_shape = struct((tokens, query_cols), BF16)
    ds_shape = struct((12, half, heads * half), BF16)
    dsp_shape = struct((6, half, heads * half), BF16)
    part_shape = struct((2, tokens, kv_cols), BF16)
    sums_shape = (1, 2, tokens, kv_cols)
    flags_shape = struct((8, tokens), jnp.int32)
    one_sum, two_sums = struct(sums_shape, F32), pltpu.VMEM((2,) + sums_shape[1:], F32)
    keys_scratch = pltpu.VMEM((2, tokens, kv_cols), BF16)
    flops = 2 * 5 * heads * tokens * tokens * HEAD_WIDTH

    q, do, flags, ds, own_sums = call(
        own_kernel,
        (block_shape, block_shape, flags_shape, ds_shape, one_sum),
        [HBM] * 3 + [VMEM] * 2,
        flops=flops,
        bytes_accessed=4 << 20,
        scratch=[
            pltpu.SMEM(offsets.shape[::-1], jnp.int32),
            pltpu.SemaphoreType.DMA,
            pltpu.SemaphoreType.DMA((2, kv_cols // HEAD_WIDTH)),
        ],
    )(in_hbm(offsets.T), in_hbm(q), in_hbm(do), rows, kv)
    mine = (flags, q, do, rows)
    other = (q_other, do_other, rows_other)
    ds, side_sums = call(
        side_kernel, (ds_shape, one_sum), [VMEM] * 6, flops=flops, bytes_accessed=4 << 20, aliases={5: 0}
    )(*mine, kv_side, ds)
    ds, ds_other, part_side, part_back, first_keys = call(
        back_kernel,
        (ds_shape, dsp_shape, part_shape, part_shape, part_shape),
        [VMEM] * 11,
        flops=flops,
        bytes_accessed=4 << 20,
        aliases={10: 0},
        scratch=[two_sums],
    )(*mine, *other, kv_side, kv_back, side_sums, ds)
    ds, ds_other, own_sums, part_far, pq = call(
        far_kernel,
        (ds_shape, dsp_shape, struct(sums_shape[1:], F32), part_shape, block_shape),
        [VMEM] * 13,
        flops=flops,
        bytes_accessed=4 << 20,
        aliases={11: 0, 12: 1},
        scratch=[keys_scratch, two_sums],
    )(*mine, *other, kv, kv_far, first_keys, own_sums, ds, ds_other)
    kvs = (kv, kv_side, kv_back, kv_far)
    back_side = moved(part_side, -FAR, 0)
    back_back = moved(part_back, 0, -BACK)
    pq_other = swapped(pq)
    back_far = moved(part_far, -FAR, -BACK)
    q_mine = call(mine_kernel, struct((2, half, query_cols), F32), [VMEM] * 5, flops=flops // 4, bytes_accessed=1 << 20)(
        ds, *kvs
    )
    rows_shape = struct((half, query_cols), BF16)
    q_keep, q_send = call(query_kernel, (rows_shape, rows_shape), [VMEM] * 2, bytes_accessed=2 << 20)(q_mine, pq_other)
    q_recv = crossed(q_send)
    kv_shape = struct((2, half, kv_cols), BF16)
    kv_keep, kv_send = call(sum_kernel, (kv_shape, kv_shape), [VMEM] * 4, bytes_accessed=1 << 20)(
        own_sums, back_far, back_back, back_side
    )
    kv_recv = crossed(kv_send)
    grad_query = call(
        join_query_kernel,
        struct((1, half, 2 * query_cols), BF16),
        [VMEM] * 2,
        out_space=HBM,
        bytes_accessed=2 << 20,
        scratch=[pltpu.SemaphoreType.DMA((1, 2))],
    )(q_keep, q_recv)
    grad_key, grad_value = call(
        join_keys_kernel,
        (struct((1, half, 2 * kv_cols), BF16),) * 2,
        [VMEM] * 2,
        out_space=HBM,
        bytes_accessed=1 << 18,
        scratch=[pltpu.SemaphoreType.DMA((2, 2))],
    )(kv_keep, kv_recv)
    return grad_query, grad_key, grad_value


def solution(mesh):
    split = P(("inner", "outer"), None, "head")
    joined = P(("inner", "outer"), "head", None)
    return jax.shard_map(
        program,
        mesh=mesh,
        in_specs=(split,) * 6 + (P(),),
        out_specs=(joined,) * 3,
        check_vma=False,
    )
```

time: 45 us -> 39.4 us (0.88)
  local copies, waits for them, and re-layouts: 4.6 us -> 0 us
  Pallas kernels: 14 us -> 10.8 us
  waiting for transfers between devices: 12.2 us -> 14.6 us
    unnamed x19 -> x0, local copies, waits for them, and re-layouts: 4.6 us -> none
    ppermute x6, waiting for transfers between devices: 5.89 us -> 9.84 us  [moved(): return lax.ppermute(value, ('inner', 'outer'), pairs)]
    pallas_call x7 -> x10, Pallas kernels: 14 us -> 10.8 us  [the longest x1 2.66 us: program(): call(own_kernel, (block_shape, block_shape, flags_shape, ds_shape, one_su...]
    ppermute x4, waiting for transfers between devices: 2.55 us -> 1 us  [swapped(): lax.ppermute(value, 'inner', [(i, i ^ 1) for i in range(lax.axis_size('in...]
    ppermute x6, starting transfers between devices: 10.3 us -> 9.67 us  [moved(): return lax.ppermute(value, ('inner', 'outer'), pairs)]
    ppermute x4, starting transfers between devices: 0.71 us -> 1.22 us  [swapped(): lax.ppermute(value, 'inner', [(i, i ^ 1) for i in range(lax.axis_size('in...]
  transfers between devices with their start and end apart: 12 -> 12, of which waited for: 5 -> 6; matrix products, arithmetic and copies ran while one was open for 0% -> 0% of each run, Pallas kernels for 16% -> 20%
where the time goes in v2:
time: 39.4 us; the launch traced here: 39.2 us
  waiting for transfers between devices  14.6 us (37%)
  starting transfers between devices  13 us (33%)
  Pallas kernels  10.8 us (27%)
  between operations  0.74 us (2%)
    ppermute x6, waiting for transfers between devices, moved(): return lax.ppermute(value, ('inner', 'outer'), pairs)  9.84 us
    ppermute x6, starting transfers between devices, moved(): return lax.ppermute(value, ('inner', 'outer'), pairs)  9.67 us
    ppermute x2, waiting for transfers between devices, crossed(): return lax.ppermute(value, 'head', [(0, 1), (1, 0)])  3.76 us
    pallas_call x1, Pallas kernels, program(): call(own_kernel, (block_shape, block_shape, flags_shape, ds_shape, one_su...  2.66 us
    ppermute x2, starting transfers between devices, crossed(): return lax.ppermute(value, 'head', [(0, 1), (1, 0)])  2.16 us
    pallas_call x1, Pallas kernels, program(): call(far_kernel, (ds_shape, dsp_shape, struct(sums_shape[1:], F32), part_...  2.12 us
    pallas_call x1, Pallas kernels, program(): call(back_kernel, (ds_shape, dsp_shape, part_shape, part_shape, part_shap...  1.86 us
    ppermute x4, starting transfers between devices, swapped(): lax.ppermute(value, 'inner', [(i, i ^ 1) for i in range(lax.axis_size('in...  1.22 us
  transfers between devices with their start and end apart: 12, of which 6 were waited for; matrix products, arithmetic and copies ran while one was open for 0% of the time, Pallas kernels for 20%

profile of v2, /device:TPU:0, one launch (start us, length us, event | category | flops | bytes accessed | tf_op | source)
XLA Modules:
  0.0 39.2 jit_solution(2082324235269380137)
XLA Ops:
  0.6 0.6 %collective-permute-start = (bf16[128,2048]{1,0:T(8,128)(2,1)}, bf16[128,2048]{1,0:T(8,128)(2,1)S(1)}, u32[]{:S(2)}, u32[]{:S(2)}) collective-permute-start(bf16[128,2048]{1,0:T(8,128)(2,1)} %bitcast.15), channel_id=1, source_target_pairs={{0,4},{4,0},{8,12},{12,8},{1,5},{5,1},{9,13},{13,9},{2,6},{6,2},{1... | collective-permute-start | bytes 1572872 | tf_op jit(solution)/shard_map/ppermute | solution.py:335
  1.2 0.1 collective-permute-start.1
  1.3 1.0 %shard_map.94 = (bf16[2,128,256]{2,1,0:T(8,128)(2,1)S(1)}, f32[2,2,8,128]{3,2,1,0:T(8,128)S(1)}) custom-call(bf16[128,256]{1,0:T(8,128)(2,1)} %bitcast.11, bf16[128,256]{1,0:T(8,128)(2,1)} %bitcast.12, f32[16,128]{1,0:T(8,128)} %bitcast.13, f32[16,128]{1,0:T(8,128)} %bitcast.14), custom_call_target="tpu_custom_call" | custom-call | bytes 262144 | tf_op jit(solution)/shard_map/pallas_call | solution.py:358
  2.3 3.0 %collective-permute-start.3 = (bf16[2,128,256]{2,1,0:T(8,128)(2,1)S(1)}, bf16[2,128,256]{2,1,0:T(8,128)(2,1)S(1)}, u32[]{:S(2)}, u32[]{:S(2)}) collective-permute-start(bf16[2,128,256]{2,1,0:T(8,128)(2,1)S(1)} %get-tuple-element.28.kv_ref.own_ref), channel_id=1, source_target_pairs={{0,1},{1,2},{2,3},{3,0},{4,5},{5,6},{6,7},{7,4},{8,9},{9,10},{10,1... | collective-permute-start | bytes 393224 | tf_op jit(solution)/shard_map/ppermute | solution.py:331
  5.3 1.5 %collective-permute-start.5 = (bf16[2,128,256]{2,1,0:T(8,128)(2,1)S(1)}, bf16[2,128,256]{2,1,0:T(8,128)(2,1)S(1)}, u32[]{:S(2)}, u32[]{:S(2)}) collective-permute-start(bf16[2,128,256]{2,1,0:T(8,128)(2,1)S(1)} %get-tuple-element.28.kv_ref.own_ref), channel_id=1, source_target_pairs={{0,8},{1,9},{2,10},{3,11},{4,12},{5,13},{6,14},{7,15},{8,0},{9,1},... | collective-permute-start | bytes 393224 | tf_op jit(solution)/shard_map/ppermute | solution.py:331
  6.8 4.3 %collective-permute-done.3.kv_ref.back_ref = bf16[2,128,256]{2,1,0:T(8,128)(2,1)S(1)} collective-permute-done((bf16[2,128,256]{2,1,0:T(8,128)(2,1)S(1)}, bf16[2,128,256]{2,1,0:T(8,128)(2,1)S(1)}, u32[]{:S(2)}, u32[]{:S(2)}) %collective-permute-start.3) | collective-permute-done | bytes 131104 | tf_op jit(solution)/shard_map/ppermute | solution.py:331
  11.1 1.5 %collective-permute-start.4 = (bf16[2,128,256]{2,1,0:T(8,128)(2,1)S(1)}, bf16[2,128,256]{2,1,0:T(8,128)(2,1)S(1)}, u32[]{:S(2)}, u32[]{:S(2)}) collective-permute-start(bf16[2,128,256]{2,1,0:T(8,128)(2,1)S(1)} %collective-permute-done.3.kv_ref.back_ref), channel_id=1, source_target_pairs={{0,8},{1,9},{2,10},{3,11},{4,12},{5,13},{6,14},{7,15},{8,0},{9,1},... | collective-permute-start | bytes 393224 | tf_op jit(solution)/shard_map/ppermute | solution.py:331
  12.6 0.0 collective-permute-start.2
  12.6 2.7 %shard_map.95 = (bf16[128,2048]{1,0:T(8,128)(2,1)S(1)}, bf16[128,2048]{1,0:T(8,128)(2,1)S(1)}, s32[8,128]{1,0:T(8,128)S(1)}, bf16[12,64,1024]{2,1,0:T(8,128)(2,1)S(1)}, f32[1,2,128,256]{3,2,1,0:T(8,128)S(1)}) custom-call(s32[2,16]{1,0:T(2,128)} %bitcast.19, bf16[128,2048]{1,0:T(8,128)(2,1)} %bitcast.16, bf16[128,2048]{1,0:T(8,128)(2,1)} %bitcast.18, ...), custom_call_target="tpu_custom_call" | custom-call | flops 335544320 | bytes 4194304 | tf_op jit(solution)/shard_map/pallas_call | solution.py:381
  15.2 0.0 collective-permute-done.5.kv_ref.side_ref
  15.2 1.0 %shard_map.96 = (bf16[12,64,1024]{2,1,0:T(8,128)(2,1)S(1)}, f32[1,2,128,256]{3,2,1,0:T(8,128)S(1)}) custom-call(s32[8,128]{1,0:T(8,128)S(1)} %get-tuple-element.29.flags_ref, bf16[128,2048]{1,0:T(8,128)(2,1)S(1)} %get-tuple-element.30.q_ref, bf16[128,2048]{1,0:T(8,128)(2,1)S(1)} %get-tuple-element.31.do_ref, ...), custom_call_target="tpu_custom_call", output_to_operand_aliasing={{0}: (5, {})} | custom-call | flops 335544320 | bytes 4194304 | tf_op jit(solution)/shard_map/pallas_call | solution.py:395
  16.2 0.0 collective-permute-done.2.rowsp_ref
  16.2 0.0 collective-permute-done.qp_ref
  16.3 0.0 collective-permute-done.1.dop_ref
  16.3 1.9 %shard_map.97 = (bf16[12,64,1024]{2,1,0:T(8,128)(2,1)S(1)}, bf16[6,64,1024]{2,1,0:T(8,128)(2,1)S(1)}, bf16[2,128,256]{2,1,0:T(8,128)(2,1)S(1)}, bf16[2,128,256]{2,1,0:T(8,128)(2,1)S(1)}, bf16[2,128,256]{2,1,0:T(8,128)(2,1)S(1)}) custom-call(s32[8,128]{1,0:T(8,128)S(1)} %get-tuple-element.29.flags_ref, ...), custom_call_target="tpu_custom_call", output_to_operand_aliasing={{0}: (10, {})} | custom-call | flops 335544320 | bytes 4194304 | tf_op jit(solution)/shard_map/pallas_call | solution.py:398
  18.1 0.0 collective-permute-done.4.kv_ref.far_ref
  18.1 2.1 %shard_map.98 = (bf16[12,64,1024]{2,1,0:T(8,128)(2,1)S(1)}, bf16[6,64,1024]{2,1,0:T(8,128)(2,1)S(1)}, f32[2,128,256]{2,1,0:T(8,128)S(1)}, bf16[2,128,256]{2,1,0:T(8,128)(2,1)S(1)}, bf16[128,2048]{1,0:T(8,128)(2,1)S(1)}) custom-call(s32[8,128]{1,0:T(8,128)S(1)} %get-tuple-element.29.flags_ref, ...), custom_call_target="tpu_custom_call", output_to_operand_aliasing={{0}: (11, {}), {1}: (12, {})} | custom-call | flops 335544320 | bytes 4194304 | tf_op jit(solution)/shard_map/pallas_call | solution.py:407
  20.3 0.6 %collective-permute-start.6 = (bf16[128,2048]{1,0:T(8,128)(2,1)S(1)}, bf16[128,2048]{1,0:T(8,128)(2,1)S(1)}, u32[]{:S(2)}, u32[]{:S(2)}) collective-permute-start(bf16[128,2048]{1,0:T(8,128)(2,1)S(1)} %get-tuple-element.40), channel_id=1, source_target_pairs={{0,4},{4,0},{8,12},{12,8},{1,5},{5,1},{9,13},{13,9},{2,6},{6,2},{1... | collective-permute-start | bytes 1572872 | tf_op jit(solution)/shard_map/ppermute | solution.py:335
  20.8 0.5 %shard_map.99.mine_ref = f32[2,64,2048]{2,1,0:T(8,128)S(1)} custom-call(bf16[12,64,1024]{2,1,0:T(8,128)(2,1)S(1)} %get-tuple-element.39.ds_ref, bf16[2,128,256]{2,1,0:T(8,128)(2,1)S(1)} %get-tuple-element.28.kv_ref.own_ref, bf16[2,128,256]{2,1,0:T(8,128)(2,1)S(1)} %collective-permute-done.5.kv_ref.side_ref, ...), custom_call_target="tpu_custom_call" | custom-call | flops 83886080 | bytes 1048576 | tf_op jit(solution)/shard_map/pallas_call | solution.py:421
  21.4 1.0 %collective-permute-done.6.recv_ref = bf16[128,2048]{1,0:T(8,128)(2,1)S(1)} collective-permute-done((bf16[128,2048]{1,0:T(8,128)(2,1)S(1)}, bf16[128,2048]{1,0:T(8,128)(2,1)S(1)}, u32[]{:S(2)}, u32[]{:S(2)}) %collective-permute-start.6) | collective-permute-done | bytes 524320 | tf_op jit(solution)/shard_map/ppermute | solution.py:335
  22.4 0.1 shard_map.100
  22.5 1.6 %collective-permute-start.7 = (bf16[64,2048]{1,0:T(8,128)(2,1)S(1)}, bf16[64,2048]{1,0:T(8,128)(2,1)S(1)}, u32[]{:S(2)}, u32[]{:S(2)}) collective-permute-start(bf16[64,2048]{1,0:T(8,128)(2,1)S(1)} %get-tuple-element.42), channel_id=1, source_target_pairs={{0,16},{16,0},{1,17},{17,1},{2,18},{18,2},{3,19},{19,3},{4,20},{20... | collective-permute-start | bytes 786440 | tf_op jit(solution)/shard_map/ppermute | solution.py:339
  24.0 1.7 %collective-permute-start.8 = (bf16[2,128,256]{2,1,0:T(8,128)(2,1)S(1)}, bf16[2,128,256]{2,1,0:T(8,128)(2,1)S(1)}, u32[]{:S(2)}, u32[]{:S(2)}) collective-permute-start(bf16[2,128,256]{2,1,0:T(8,128)(2,1)S(1)} %get-tuple-element.44), channel_id=1, source_target_pairs={{0,11},{1,8},{2,9},{3,10},{4,15},{5,12},{6,13},{7,14},{8,3},{9,0},... | collective-permute-start | bytes 393224 | tf_op jit(solution)/shard_map/ppermute | solution.py:331
  25.8 0.4 %collective-permute-start.9 = (bf16[2,128,256]{2,1,0:T(8,128)(2,1)S(1)}, bf16[2,128,256]{2,1,0:T(8,128)(2,1)S(1)}, u32[]{:S(2)}, u32[]{:S(2)}) collective-permute-start(bf16[2,128,256]{2,1,0:T(8,128)(2,1)S(1)} %get-tuple-element.45), channel_id=1, source_target_pairs={{0,3},{1,0},{2,1},{3,2},{4,7},{5,4},{6,5},{7,6},{8,11},{9,8},{10,9... | collective-permute-start | bytes 393224 | tf_op jit(solution)/shard_map/ppermute | solution.py:331
  26.2 1.5 %collective-permute-start.10 = (bf16[2,128,256]{2,1,0:T(8,128)(2,1)S(1)}, bf16[2,128,256]{2,1,0:T(8,128)(2,1)S(1)}, u32[]{:S(2)}, u32[]{:S(2)}) collective-permute-start(bf16[2,128,256]{2,1,0:T(8,128)(2,1)S(1)} %get-tuple-element.46), channel_id=1, source_target_pairs={{0,8},{1,9},{2,10},{3,11},{4,12},{5,13},{6,14},{7,15},{8,0},{9,1},... | collective-permute-start | bytes 393224 | tf_op jit(solution)/shard_map/ppermute | solution.py:331
  27.7 3.6 %collective-permute-done.8.a_ref = bf16[2,128,256]{2,1,0:T(8,128)(2,1)S(1)} collective-permute-done((bf16[2,128,256]{2,1,0:T(8,128)(2,1)S(1)}, bf16[2,128,256]{2,1,0:T(8,128)(2,1)S(1)}, u32[]{:S(2)}, u32[]{:S(2)}) %collective-permute-start.8) | collective-permute-done | bytes 131104 | tf_op jit(solution)/shard_map/ppermute | solution.py:331
  31.3 1.0 %collective-permute-done.9.b_ref = bf16[2,128,256]{2,1,0:T(8,128)(2,1)S(1)} collective-permute-done((bf16[2,128,256]{2,1,0:T(8,128)(2,1)S(1)}, bf16[2,128,256]{2,1,0:T(8,128)(2,1)S(1)}, u32[]{:S(2)}, u32[]{:S(2)}) %collective-permute-start.9) | collective-permute-done | bytes 131104 | tf_op jit(solution)/shard_map/ppermute | solution.py:331
  32.3 0.9 %collective-permute-done.10.c_ref = bf16[2,128,256]{2,1,0:T(8,128)(2,1)S(1)} collective-permute-done((bf16[2,128,256]{2,1,0:T(8,128)(2,1)S(1)}, bf16[2,128,256]{2,1,0:T(8,128)(2,1)S(1)}, u32[]{:S(2)}, u32[]{:S(2)}) %collective-permute-start.10) | collective-permute-done | bytes 131104 | tf_op jit(solution)/shard_map/ppermute | solution.py:331
  33.3 0.1 shard_map.102
  33.3 0.6 %collective-permute-start.11 = (bf16[2,64,256]{2,1,0:T(8,128)(2,1)S(1)}, bf16[2,64,256]{2,1,0:T(8,128)(2,1)S(1)}, u32[]{:S(2)}, u32[]{:S(2)}) collective-permute-start(bf16[2,64,256]{2,1,0:T(8,128)(2,1)S(1)} %get-tuple-element.48), channel_id=1, source_target_pairs={{0,16},{16,0},{1,17},{17,1},{2,18},{18,2},{3,19},{19,3},{4,20},{20... | collective-permute-start | bytes 196616 | tf_op jit(solution)/shard_map/ppermute | solution.py:339
  33.9 3.8 %collective-permute-done.11.received = bf16[2,64,256]{2,1,0:T(8,128)(2,1)S(1)} collective-permute-done((bf16[2,64,256]{2,1,0:T(8,128)(2,1)S(1)}, bf16[2,64,256]{2,1,0:T(8,128)(2,1)S(1)}, u32[]{:S(2)}, u32[]{:S(2)}) %collective-permute-start.11) | collective-permute-done | bytes 65568 | tf_op jit(solution)/shard_map/ppermute | solution.py:339
  37.7 0.7 %shard_map.103 = (bf16[1,64,512]{2,1,0:T(8,128)(2,1)}, bf16[1,64,512]{2,1,0:T(8,128)(2,1)}) custom-call(bf16[2,64,256]{2,1,0:T(8,128)(2,1)S(1)} %get-tuple-element.47.kept, bf16[2,64,256]{2,1,0:T(8,128)(2,1)S(1)} %collective-permute-done.11.received), custom_call_target="tpu_custom_call" | custom-call | bytes 262144 | tf_op jit(solution)/shard_map/pallas_call | solution.py:440
  38.3 0.0 collective-permute-done.7.received
  38.4 0.8 %shard_map.101 = bf16[1,64,4096]{2,1,0:T(8,128)(2,1)} custom-call(bf16[64,2048]{1,0:T(8,128)(2,1)S(1)} %get-tuple-element.41.kept, bf16[64,2048]{1,0:T(8,128)(2,1)S(1)} %collective-permute-done.7.received), custom_call_target="tpu_custom_call" | custom-call | bytes 2097152 | tf_op jit(solution)/shard_map/pallas_call | solution.py:432
Async XLA Ops:
  0.6 15.6 %collective-permute-start = (bf16[128,2048]{1,0:T(8,128)(2,1)}, bf16[128,2048]{1,0:T(8,128)(2,1)S(1)}, u32[]{:S(2)}, u32[]{:S(2)}) collective-permute-start(bf16[128,2048]{1,0:T(8,128)(2,1)} %bitcast.15), channel_id=1, source_target_pairs={{0,4},{4,0},{8,12},{12,8},{1,5},{5,1},{9,13},{13,9},{2,6},{6,2},{1... | collective-permute-start | bytes 1572872 | tf_op jit(solution)/shard_map/ppermute | solution.py:335
  1.2 15.1 %collective-permute-start.1 = (bf16[128,2048]{1,0:T(8,128)(2,1)}, bf16[128,2048]{1,0:T(8,128)(2,1)S(1)}, u32[]{:S(2)}, u32[]{:S(2)}) collective-permute-start(bf16[128,2048]{1,0:T(8,128)(2,1)} %bitcast.17), channel_id=1, source_target_pairs={{0,4},{4,0},{8,12},{12,8},{1,5},{5,1},{9,13},{13,9},{2,6},{6,2},{1... | collective-permute-start | bytes 1572872 | tf_op jit(solution)/shard_map/ppermute | solution.py:335
  2.3 8.8 %collective-permute-start.3 = (bf16[2,128,256]{2,1,0:T(8,128)(2,1)S(1)}, bf16[2,128,256]{2,1,0:T(8,128)(2,1)S(1)}, u32[]{:S(2)}, u32[]{:S(2)}) collective-permute-start(bf16[2,128,256]{2,1,0:T(8,128)(2,1)S(1)} %get-tuple-element.28.kv_ref.own_ref), channel_id=1, source_target_pairs={{0,1},{1,2},{2,3},{3,0},{4,5},{5,6},{6,7},{7,4},{8,9},{9,10},{10,1... | collective-permute-start | bytes 393224 | tf_op jit(solution)/shard_map/ppermute | solution.py:331
  5.3 9.9 %collective-permute-start.5 = (bf16[2,128,256]{2,1,0:T(8,128)(2,1)S(1)}, bf16[2,128,256]{2,1,0:T(8,128)(2,1)S(1)}, u32[]{:S(2)}, u32[]{:S(2)}) collective-permute-start(bf16[2,128,256]{2,1,0:T(8,128)(2,1)S(1)} %get-tuple-element.28.kv_ref.own_ref), channel_id=1, source_target_pairs={{0,8},{1,9},{2,10},{3,11},{4,12},{5,13},{6,14},{7,15},{8,0},{9,1},... | collective-permute-start | bytes 393224 | tf_op jit(solution)/shard_map/ppermute | solution.py:331
  11.1 7.1 %collective-permute-start.4 = (bf16[2,128,256]{2,1,0:T(8,128)(2,1)S(1)}, bf16[2,128,256]{2,1,0:T(8,128)(2,1)S(1)}, u32[]{:S(2)}, u32[]{:S(2)}) collective-permute-start(bf16[2,128,256]{2,1,0:T(8,128)(2,1)S(1)} %collective-permute-done.3.kv_ref.back_ref), channel_id=1, source_target_pairs={{0,8},{1,9},{2,10},{3,11},{4,12},{5,13},{6,14},{7,15},{8,0},{9,1},... | collective-permute-start | bytes 393224 | tf_op jit(solution)/shard_map/ppermute | solution.py:331
  12.6 3.7 %collective-permute-start.2 = (f32[2,2,8,128]{3,2,1,0:T(8,128)S(1)}, f32[2,2,8,128]{3,2,1,0:T(8,128)S(1)}, u32[]{:S(2)}, u32[]{:S(2)}) collective-permute-start(f32[2,2,8,128]{3,2,1,0:T(8,128)S(1)} %get-tuple-element.27.rows_ref), channel_id=1, source_target_pairs={{0,4},{4,0},{8,12},{12,8},{1,5},{5,1},{9,13},{13,9},{2,6},{6,2},{1... | collective-permute-start | bytes 49160 | tf_op jit(solution)/shard_map/ppermute | solution.py:335
  20.3 2.1 %collective-permute-start.6 = (bf16[128,2048]{1,0:T(8,128)(2,1)S(1)}, bf16[128,2048]{1,0:T(8,128)(2,1)S(1)}, u32[]{:S(2)}, u32[]{:S(2)}) collective-permute-start(bf16[128,2048]{1,0:T(8,128)(2,1)S(1)} %get-tuple-element.40), channel_id=1, source_target_pairs={{0,4},{4,0},{8,12},{12,8},{1,5},{5,1},{9,13},{13,9},{2,6},{6,2},{1... | collective-permute-start | bytes 1572872 | tf_op jit(solution)/shard_map/ppermute | solution.py:335
  22.5 15.9 %collective-permute-start.7 = (bf16[64,2048]{1,0:T(8,128)(2,1)S(1)}, bf16[64,2048]{1,0:T(8,128)(2,1)S(1)}, u32[]{:S(2)}, u32[]{:S(2)}) collective-permute-start(bf16[64,2048]{1,0:T(8,128)(2,1)S(1)} %get-tuple-element.42), channel_id=1, source_target_pairs={{0,16},{16,0},{1,17},{17,1},{2,18},{18,2},{3,19},{19,3},{4,20},{20... | collective-permute-start | bytes 786440 | tf_op jit(solution)/shard_map/ppermute | solution.py:339
  24.0 7.3 %collective-permute-start.8 = (bf16[2,128,256]{2,1,0:T(8,128)(2,1)S(1)}, bf16[2,128,256]{2,1,0:T(8,128)(2,1)S(1)}, u32[]{:S(2)}, u32[]{:S(2)}) collective-permute-start(bf16[2,128,256]{2,1,0:T(8,128)(2,1)S(1)} %get-tuple-element.44), channel_id=1, source_target_pairs={{0,11},{1,8},{2,9},{3,10},{4,15},{5,12},{6,13},{7,14},{8,3},{9,0},... | collective-permute-start | bytes 393224 | tf_op jit(solution)/shard_map/ppermute | solution.py:331
  25.8 6.6 %collective-permute-start.9 = (bf16[2,128,256]{2,1,0:T(8,128)(2,1)S(1)}, bf16[2,128,256]{2,1,0:T(8,128)(2,1)S(1)}, u32[]{:S(2)}, u32[]{:S(2)}) collective-permute-start(bf16[2,128,256]{2,1,0:T(8,128)(2,1)S(1)} %get-tuple-element.45), channel_id=1, source_target_pairs={{0,3},{1,0},{2,1},{3,2},{4,7},{5,4},{6,5},{7,6},{8,11},{9,8},{10,9... | collective-permute-start | bytes 393224 | tf_op jit(solution)/shard_map/ppermute | solution.py:331
  26.2 7.0 %collective-permute-start.10 = (bf16[2,128,256]{2,1,0:T(8,128)(2,1)S(1)}, bf16[2,128,256]{2,1,0:T(8,128)(2,1)S(1)}, u32[]{:S(2)}, u32[]{:S(2)}) collective-permute-start(bf16[2,128,256]{2,1,0:T(8,128)(2,1)S(1)} %get-tuple-element.46), channel_id=1, source_target_pairs={{0,8},{1,9},{2,10},{3,11},{4,12},{5,13},{6,14},{7,15},{8,0},{9,1},... | collective-permute-start | bytes 393224 | tf_op jit(solution)/shard_map/ppermute | solution.py:331
  33.3 4.3 %collective-permute-start.11 = (bf16[2,64,256]{2,1,0:T(8,128)(2,1)S(1)}, bf16[2,64,256]{2,1,0:T(8,128)(2,1)S(1)}, u32[]{:S(2)}, u32[]{:S(2)}) collective-permute-start(bf16[2,64,256]{2,1,0:T(8,128)(2,1)S(1)} %get-tuple-element.48), channel_id=1, source_target_pairs={{0,16},{16,0},{1,17},{17,1},{2,18},{18,2},{3,19},{19,3},{4,20},{20... | collective-permute-start | bytes 196616 | tf_op jit(solution)/shard_map/ppermute | solution.py:339
